TPU v7x, 32 devices: a whole 2x2x4 slice. The times are simulated.
32 devices in a mesh: dp: 8 (over z, core), mp: 4 (over y, x).
Axes of the slice: x: 2, y: 2, z: 4, core: 2. Of those that a mesh axis runs over, the one named last changes fastest.
Arguments:
- inputs: bfloat16 [1024, 32768], P('dp', 'mp'), may hold values from -6 to 6
- cotangent: bfloat16 [1024, 32768], P('dp', 'mp'), may hold values from -6 to 6
- first_weight: bfloat16 [128, 2, 256, 256], P('mp', None, 'dp'), may hold values from -0.25 to 0.25
- second_weight: bfloat16 [128, 2, 256, 256], P('mp', None, 'dp'), may hold values from -0.25 to 0.25
- orders: int32 [2, 256], replicated, may hold values from 0 to 255, each once within a row
Outputs:
- input_grad: bfloat16 [1024, 32768], P('dp', 'mp')
- first_grad: float32 [128, 2, 256, 256], P('mp', None, 'dp')
- second_grad: float32 [128, 2, 256, 256], P('mp', None, 'dp')
Inputs may be any that keep to these rules, and one draw needn't show every extreme that they name: Each of the two rows of orders is a permutation of 0 to 255.
All inputs are finite; a program needn't handle non-finite values.
Results may differ from a plain program's by a relative error of at most 0.018.
Values may be sent and summed in bfloat16 or wider, within the bound.
A program may use at most 128 MiB of HBM per device.

v0:
```python
import functools
import math

import jax
import jax.numpy as jnp
from jax import lax
from jax.experimental import pallas as pl
from jax.experimental.pallas import tpu as pltpu
from jax.sharding import PartitionSpec as P

B = 256
MESH = pl.DeviceIdType.MESH
ANY = pl.BlockSpec(memory_space=pl.ANY)
NT = (((1,), (1,)), ((), ()))
TN = (((0,), (0,)), ((), ()))


class Plan:
    def __init__(self, dp, mp, local_blocks):
        self.dp, self.mp, self.nb = dp, mp, local_blocks
        self.low = mp // 4
        g = max(1, dp // 2)
        while local_blocks % (4 * g):
            g //= 2
        self.g, self.groups = g, dp // g
        self.nq = local_blocks // (4 * g)

    def here(self):
        d, m = lax.axis_index("dp"), lax.axis_index("mp")
        return d, d // self.g, d % self.g, m // self.low, m % self.low


def greet(plan, d, h, lo):
    barrier = pltpu.get_barrier_semaphore()
    others = 4 * plan.dp
    me = d * 4 + h
    for k in range(1, others):
        t = (me + k) % others
        pl.semaphore_signal(
            barrier, inc=1, device_id=(t // 4, (t % 4) * plan.low + lo), device_id_type=MESH
        )
    pl.semaphore_wait(barrier, others - 1)


def sweep(first, last, body):
    lax.fori_loop(first, last, lambda k, _: (body(k), None)[1], None)


def whole(plan, scale, order, x, c, w1, w2, igo, gfo, gso, xb, cb, w1b, w2b, ig, gf, gs, w1p, w2p, act, pre,
          ts, tr, ws, wr, ls, os, orr, gsem, gr, ol):
    d, gi, r, h, lo = plan.here()
    tok, rows, nq = x.shape[0], w1.shape[2], plan.nq
    n_t, n_w = 4 * plan.g, 4 * plan.dp
    me_o, me_w = r * 4 + h, d * 4 + h
    greet(plan, d, h, lo)

    def peer_of_group(t):
        return (gi * plan.g + t // 4, (t % 4) * plan.low + lo)

    def peer_of_all(t):
        return (t // 4, (t % 4) * plan.low + lo)

    def tokens_in(i, a, k):
        t = (me_o + 5 * k) % n_t
        src, dst = ((x, xb), (c, cb))[a]
        s = src.at[:, pl.ds(pl.multiple_of((t * nq + i) * B, B), B)]
        e = dst.at[i, h, pl.ds(pl.multiple_of(r * tok, tok), tok)]
        if isinstance(k, int) and k == 0:
            return pltpu.make_async_copy(s, e, ls.at[i, a])
        return pltpu.make_async_remote_copy(
            s, e, ts.at[i, a, k], tr.at[i, a, k], device_id=peer_of_group(t), device_id_type=MESH
        )

    def weights_in(i, a, k):
        t = (me_w + 11 * k) % n_w
        src, dst = ((w1, w1b), (w2, w2b))[a]
        o = ((t // 4) % plan.g) * 4 + t % 4
        s = src.at[o * nq + i]
        e = dst.at[i, h, :, pl.ds(pl.multiple_of(d * rows, rows), rows)]
        if isinstance(k, int) and k == 0:
            return pltpu.make_async_copy(s, e, ls.at[i, 2 + a])
        return pltpu.make_async_remote_copy(
            s, e, ws.at[i, a, k], wr.at[i, a, k], device_id=peer_of_all(t), device_id_type=MESH
        )

    def tokens_out(i, k):
        t = (me_o + 5 * k) % n_t
        s = ig.at[i, t % 4, pl.ds(pl.multiple_of((t // 4) * tok, tok), tok)]
        e = igo.at[:, pl.ds(pl.multiple_of((me_o * nq + i) * B, B), B)]
        if isinstance(k, int) and k == 0:
            return pltpu.make_async_copy(s, e, ol.at[i, 0])
        return pltpu.make_async_remote_copy(
            s, e, os.at[i, k], orr.at[i, k], device_id=peer_of_group(t), device_id_type=MESH
        )

    def grads_out(i, a, k):
        t = (me_w + 11 * k) % n_w
        src, dst = ((gf, gfo), (gs, gso))[a]
        s = src.at[i, t % 4, :, pl.ds(pl.multiple_of((t // 4) * rows, rows), rows)]
        e = dst.at[gi, me_o * nq + i]
        if isinstance(k, int) and k == 0:
            return pltpu.make_async_copy(s, e, ol.at[i, 1 + a])
        return pltpu.make_async_remote_copy(
            s, e, gsem.at[i, a, k], gr.at[i, a, k], device_id=peer_of_all(t), device_id_type=MESH
        )

    def all_in(i, act_on):
        def some_weights(k, first):
            for j in range(first, plan.groups):
                for a in (0, 1):
                    act_on(weights_in(i, a, plan.groups * k + j))

        def both(k):
            act_on(tokens_in(i, 0, k))
            some_weights(k, 0)
            act_on(tokens_in(i, 1, k))

        some_weights(0, 1)
        sweep(1, n_t, both)

    def all_out(i, act_on):
        def some_grads(k, first):
            for j in range(first, plan.groups):
                for a in (0, 1):
                    act_on(grads_out(i, a, plan.groups * k + j))

        def both(k):
            act_on(tokens_out(i, k))
            some_grads(k, 0)

        some_grads(0, 1)
        sweep(1, n_t, both)

    def own_in(i):
        return [f(i, a, 0) for f in (tokens_in, weights_in) for a in (0, 1)]

    def own_out(i):
        return [tokens_out(i, 0), grads_out(i, 0, 0), grads_out(i, 1, 0)]

    for i in range(nq):
        all_in(i, lambda copy: copy.start())
        for copy in own_in(i):
            copy.start()
    for i in range(nq):
        for copy in own_in(i):
            copy.wait()
        all_in(i, lambda copy: copy.wait_recv())
        factors(scale, order, xb.at[i], cb.at[i], w1b.at[i], w2b.at[i], ig.at[i], gf.at[i], gs.at[i], w1p, w2p, act, pre)
        all_out(i, lambda copy: copy.start())
        for copy in own_out(i):
            copy.start()
    for i in range(nq):
        all_in(i, lambda copy: copy.wait_send())
        for copy in own_out(i):
            copy.wait()
        all_out(i, lambda copy: copy.wait())


def dot(left, right, dims=(((1,), (0,)), ((), ()))):
    return lax.dot_general(left, right, dims, preferred_element_type=jnp.float32)


def factors(scale, order, x, c, w1, w2, ig, gf, gs, w1p, w2p, act, pre):
    bf = jnp.bfloat16
    place = lax.broadcasted_iota(jnp.int32, (B, B), 0)
    spread_one = (place == order[0:1, :]).astype(jnp.float32).astype(bf)
    spread_two = (place == order[1:2, :]).astype(jnp.float32).astype(bf)
    root = math.sqrt(2.0 / math.pi)
    for h in range(4):
        w1p[h] = dot(spread_one, w1[h, 1]).astype(bf)
        w2p[h] = dot(spread_two, w2[h, 1]).astype(bf)
    for h in range(4):
        p, q = h ^ 2, h ^ 1
        v = dot(x[h], w1[h, 0]) + dot(x[p], w1p[h])
        up = dot(c[h], w2[h, 0], NT) + dot(c[q], w2p[q], NT)
        v2 = v * v
        t = jnp.tanh(root * v * (1.0 + 0.044715 * v2))
        half = 0.5 + 0.5 * t
        act[h] = (v * half).astype(bf)
        slope = half + (0.5 * root) * v * (1.0 - t * t) * (1.0 + (3 * 0.044715) * v2)
        pre[h] = (up * slope).astype(bf)
    for h in range(4):
        p, q = h ^ 2, h ^ 1
        ig[h] = (dot(pre[h], w1[h, 0], NT) + dot(pre[p], w1p[p], NT)).astype(bf)
        gf[h, 0] = (dot(x[h], pre[h], TN) * scale).astype(bf)
        cross = (dot(x[p], pre[h], TN) * scale).astype(bf)
        gf[h, 1] = dot(spread_one, cross, TN).astype(bf)
        gs[h, 0] = (dot(act[h], c[h], TN) * scale).astype(bf)
        cross = (dot(act[q], c[h], TN) * scale).astype(bf)
        gs[h, 1] = dot(spread_two, cross, TN).astype(bf)


def shards(plan, inputs, cotangent, first_weight, second_weight, orders):
    tok, width = inputs.shape
    rows = first_weight.shape[2]
    bf = jnp.bfloat16
    all_tok = plan.g * tok
    nq = plan.nq
    scale = 1.0 / math.sqrt(tok * plan.dp)
    dma = pltpu.SemaphoreType.DMA
    n_t, n_w = 4 * plan.g, 4 * plan.dp
    toks = pltpu.VMEM((nq, 4, all_tok, B), bf)
    mats = pltpu.VMEM((nq, 4, 2, B, B), bf)
    part = jax.ShapeDtypeStruct((plan.groups, plan.nb, 2, rows, B), bf)
    input_grad, first, second = pl.pallas_call(
        functools.partial(whole, plan, scale),
        out_shape=(jax.ShapeDtypeStruct((tok, width), bf), part, part),
        in_specs=[pl.BlockSpec(memory_space=pltpu.VMEM)] + [ANY] * 4,
        out_specs=(ANY,) * 3,
        scratch_shapes=[toks, toks, mats, mats, toks, mats, mats]
        + [pltpu.VMEM((4, B, B), bf)] * 2
        + [pltpu.VMEM((4, all_tok, B), bf)] * 2
        + [dma((nq, 2, n_t)), dma((nq, 2, n_t)), dma((nq, 2, n_w)), dma((nq, 2, n_w)), dma((nq, 4))]
        + [dma((nq, n_t)), dma((nq, n_t)), dma((nq, 2, n_w)), dma((nq, 2, n_w)), dma((nq, 3))],
        compiler_params=pltpu.CompilerParams(
            collective_id=0, has_side_effects=True, vmem_limit_bytes=56 * 2**20
        ),
        name="whole",
    )(orders, inputs, cotangent, first_weight, second_weight)
    total = lambda parts: jnp.sum(parts.astype(jnp.float32), axis=0)
    return input_grad, total(first), total(second)


def solution(mesh):
    in_specs = (
        P("dp", "mp"),
        P("dp", "mp"),
        P("mp", None, "dp", None),
        P("mp", None, "dp", None),
        P(),
    )
    out_specs = (P("dp", "mp"), P("mp", None, "dp", None), P("mp", None, "dp", None))

    def body(inputs, *rest):
        plan = Plan(mesh.shape["dp"], mesh.shape["mp"], inputs.shape[1] // B)
        return shards(plan, inputs, *rest)

    return jax.shard_map(body, mesh=mesh, in_specs=in_specs, out_specs=out_specs, check_vma=False)
```

profile of v0, /device:TPU:9, one launch (start us, length us, event | category | flops | bytes accessed | tf_op | source)
XLA Modules:
  0.0 225.8 jit_solution(8117584210004452298)
XLA Ops:
  0.6 217.9 %whole.1 = (bf16[128,8192]{1,0:T(8,128)(2,1)}, bf16[2,32,2,32,256]{4,3,2,1,0:T(8,128)(2,1)}, bf16[2,32,2,32,256]{4,3,2,1,0:T(8,128)(2,1)}) custom-call(s32[2,256]{1,0:T(2,128)} %order.1, bf16[128,8192]{1,0:T(8,128)(2,1)} %x.1, bf16[128,8192]{1,0:T(8,128)(2,1)} %c.1, bf16[32,2,32,256]{3,2,1,0:T(8,128)(2,1)} %w1.1, bf16[32,2,32,256]{3,2,1,0:T(8,128)(2,1)} %w2.1), custom_call_target="tpu_custom_call" | custom-call | tf_op jit(solution)/shard_map/whole/pallas_call | solution.py:205
  218.6 0.0 copy-start
  218.6 5.9 %convert_reduce_fusion = (f32[32,2,32,256]{3,2,1,0:T(8,128)}, f32[32,2,32,256]{3,2,1,0:T(8,128)}) fusion(bf16[2,32,2,32,256]{4,3,2,1,0:T(8,128)(2,1)} %get-tuple-element.8, bf16[2,32,2,32,256]{4,3,2,1,0:T(8,128)(2,1)} %get-tuple-element.7), kind=kLoop, calls=%fused_computation | loop fusion | flops 3145728 | bytes 8388608 | tf_op jit(solution)/shard_map/reduce_sum | solution.py:220
  224.5 0.0 copy-done
  224.5 1.3 copy.9
Async XLA Ops:
  218.6 5.9 %copy-start = (bf16[128,8192]{1,0:T(8,128)(2,1)S(1)}, bf16[128,8192]{1,0:T(8,128)(2,1)}, u32[]{:S(2)}) copy-start(bf16[128,8192]{1,0:T(8,128)(2,1)} %get-tuple-element.14) | copy-start | bytes 6291460
where the time goes:
time: 227 us; the launch traced here: 226 us
  Pallas kernels  218 us (96%)
  other arithmetic  5.88 us (3%)
    pallas_call x1, Pallas kernels, shards(): pl.pallas_call(functools.partial(whole, plan, scale), out_shape=(jax.Shap...  218 us
    reduce_sum x1, other arithmetic, shards(): total = lambda parts: jnp.sum(parts.astype(jnp.float32), axis=0)  5.88 us

commit v1 on v0

--- a/solution.py
+++ b/solution.py
@@ -154,6 +154,265 @@
         for copy in own_out(i):
             copy.wait()
         all_out(i, lambda copy: copy.wait())
+
+
+class Lanes:
+    def __init__(self, dp, mp, local_blocks):
+        self.nc = nc = dp // 4
+        self.low = mp // 4
+        self.ng = local_blocks // (4 * nc) if nc else 0
+        self.fits = dp % 4 == 0 and mp % 4 == 0 and self.ng > 0 and local_blocks % (4 * nc) == 0
+
+
+def lanes(plan, scale, order, x, c, w1, w2, igo, gfo, gso, xb, cb, w1b, w2b, ig, gf, gs, gif, gis, w1p, w2p, act, pre,
+          tin, win, wout, wrel, gin, done, st, sw, sd, sr, so, su, si, sg, sf):
+    nc, low, ng = plan.nc, plan.low, plan.ng
+    tok, rows = x.shape[0], w1.shape[2]
+    d, m = lax.axis_index("dp"), lax.axis_index("mp")
+    h, lo = m // low, m % low
+    quarter, side, core, slot = d // nc, d // (2 * nc), d % nc, d % (2 * nc)
+    inner = jnp.logical_or(quarter == 1, quarter == 2)
+    outer = jnp.logical_not(inner)
+    base, other, far = nc + side * nc, 2 * nc - side * nc, 3 * nc * side
+    first, me, us = 2 * nc * side, core * 4 + h, slot * 4 + h
+    n_s, n_o = 4 * nc, 8 * nc
+    X, W, G, GI, GO = (x, c), (w1, w2), (gf, gs), (gif, gis), (gfo, gso)
+    XB, WB = (xb, cb), (w1b, w2b)
+
+    def mp_of(hh):
+        return hh * low + lo
+
+    def span(start, size):
+        return pl.ds(pl.multiple_of(start * size, size), size)
+
+    def put(src, dst, ssem, rsem, dev):
+        return pltpu.make_async_remote_copy(src, dst, ssem, rsem, device_id=dev, device_id_type=MESH)
+
+    def arrived(ref, sem):
+        pltpu.make_async_copy(ref, ref, sem).wait()
+
+    barrier = pltpu.get_barrier_semaphore()
+
+    def hello(dev):
+        pl.semaphore_signal(barrier, inc=1, device_id=dev, device_id_type=MESH)
+
+    @pl.when(inner)
+    def _():
+        for k in range(1, n_o):
+            u = (us + k) % n_o
+            hello((first + u // 4, mp_of(u % 4)))
+        for cs in range(nc):
+            hello((other + cs, m))
+        pl.semaphore_wait(barrier, n_o - 1 + nc)
+
+    @pl.when(outer)
+    def _():
+        for k in range(n_s):
+            t = (me + k) % n_s
+            hello((base + t // 4, mp_of(t % 4)))
+        for kh in range(1, 4):
+            hello((d, mp_of((h + kh) % 4)))
+        pl.semaphore_wait(barrier, n_s + 3)
+
+    def block_of(a, t, i):
+        return W[a].at[t * ng + i]
+
+    def columns_of(a, t, i):
+        return X[a].at[:, span(t * ng + i, B)]
+
+    def own_w(i, a, k):
+        t = (me + k) % n_s
+        e = WB[a].at[i, h, :, span(d, rows)]
+        if isinstance(k, int) and k == 0:
+            return pltpu.make_async_copy(block_of(a, t, i), e, win.at[i, a, h])
+        return put(block_of(a, t, i), e, sw.at[i, a, k], win.at[i, a, h], (base + t // 4, mp_of(t % 4)))
+
+    def cross_w(i, a, cs):
+        e = WB[a].at[i, h, :, span(d, rows)]
+        return put(block_of(a, cs * 4 + h, i), e, sd.at[i, a, cs], wrel.at[i, a], (other + cs, m))
+
+    def own_t(i, a, k):
+        t = (me + k) % n_s
+        e = XB[a].at[i, h, span(slot, tok)]
+        if isinstance(k, int) and k == 0:
+            return pltpu.make_async_copy(columns_of(a, t, i), e, tin.at[i, a])
+        return put(columns_of(a, t, i), e, st.at[i, a, k], tin.at[i, a], (base + t // 4, mp_of(t % 4)))
+
+    def plane_w(i, a, cs, kh):
+        hh = (h + kh) % 4
+        s, e = block_of(a, cs * 4 + hh, i), WB[a].at[i, h, :, span(cs, rows)]
+        if kh == 0:
+            return pltpu.make_async_copy(s, e, wout.at[i, a])
+        return put(s, e, sw.at[i, a, cs * 4 + kh], wout.at[i, a], (d, mp_of(hh)))
+
+    def plane_t(i, a, cs, kh):
+        hh = (h + kh) % 4
+        s, e = columns_of(a, cs * 4 + hh, i), XB[a].at[i, h, span(cs, tok)]
+        if kh == 0:
+            return pltpu.make_async_copy(s, e, tin.at[i, a])
+        return put(s, e, st.at[i, a, cs * 4 + kh], tin.at[i, a], (d, mp_of(hh)))
+
+    def up_w(i, a, cs):
+        s, e = WB[a].at[i, :, :, span(cs, rows)], WB[a].at[i, :, :, span(d, rows)]
+        return put(s, e, su.at[i, a, cs], wout.at[i, a], (base + cs, m))
+
+    def up_t(i, a, cs):
+        s, e = XB[a].at[i, :, span(cs, tok)], XB[a].at[i, :, span(slot, tok)]
+        return put(s, e, su.at[i, 2 + a, cs], tin.at[i, a], (base + cs, m))
+
+    def relay_in(i, a, kh):
+        s = WB[a].at[i, (h + kh) % 4, :, span(base // nc, nc * rows)]
+        return put(s, s, sr.at[i, a, kh], wrel.at[i, a], (other + core, m))
+
+    def relay_out(i, a):
+        s = WB[a].at[i, :, :, span(far // nc, nc * rows)]
+        return put(s, s, so.at[i, a], wrel.at[i, a], (other + core, m))
+
+    def tokens_out(i, k):
+        u = (us + k) % n_o
+        s, e = ig.at[i, u % 4, span(u // 4, tok)], igo.at[:, span(me * ng + i, B)]
+        if isinstance(k, int) and k == 0:
+            return pltpu.make_async_copy(s, e, done.at[0])
+        return put(s, e, si.at[i, k], done.at[0], (first + u // 4, mp_of(u % 4)))
+
+    def partial(i, a, kh):
+        hh = (h + kh) % 4
+        s = G[a].at[i, hh, :, span(1 - side, 2 * nc * rows)]
+        return put(s, GI[a].at[i, hh], sg.at[i, a, kh], gin.at[i, a, kh], (other + core, m))
+
+    def grads_out(i, a, kh, k):
+        hh, r = (h + kh) % 4, (slot + k) % (2 * nc)
+        s, e = GI[a].at[i, hh, :, span(r, rows)], GO[a].at[me * ng + i]
+        if kh == 0 and k == 0:
+            return pltpu.make_async_copy(s, e, done.at[1 + a])
+        return put(s, e, sf.at[i, a, kh, k], done.at[1 + a], (first + r, mp_of(hh)))
+
+    def both(f, *at):
+        return [f(at[0], a, *at[1:]) for a in (0, 1)]
+
+    def begin(copies):
+        for copy in copies:
+            copy.start()
+
+    def combine(i):
+        for kh in range(4):
+            hh = (h + kh) % 4
+            for a in (0, 1):
+                arrived(GI[a].at[i, hh], gin.at[i, a, kh])
+                mine = G[a][i, hh, :, span(side, 2 * nc * rows)].astype(jnp.float32)
+                GI[a][i, hh] = (mine + GI[a][i, hh].astype(jnp.float32)).astype(jnp.bfloat16)
+                begin([grads_out(i, a, kh, k) for k in range(2 * nc)])
+
+    @pl.when(inner)
+    def _():
+        for i in range(ng):
+            for cs in range(nc):
+                begin(both(cross_w, i, cs))
+        for i in range(ng):
+            sweep(1, n_s, lambda k: begin(both(own_w, i, k)))
+            begin(both(own_w, i, 0))
+        for i in range(ng):
+            sweep(1, n_s, lambda k: begin(both(own_t, i, k)))
+            begin(both(own_t, i, 0))
+        for i in range(ng):
+            for kh in range(4):
+                for a in (0, 1):
+                    hh = (h + kh) % 4
+                    arrived(WB[a].at[i, hh, :, span(base // nc, nc * rows)], win.at[i, a, hh])
+                    if kh:
+                        relay_in(i, a, kh).start()
+        for i in range(ng):
+            for a in (0, 1):
+                arrived(WB[a].at[i, :, :, span(far // nc, nc * rows)], wout.at[i, a])
+                relay_out(i, a).start()
+        for i in range(ng):
+            for a in (0, 1):
+                arrived(WB[a].at[i, :, :, span(1 - side, 2 * nc * rows)], wrel.at[i, a])
+                arrived(XB[a].at[i], tin.at[i, a])
+            factors(scale, order, xb.at[i], cb.at[i], w1b.at[i], w2b.at[i], ig.at[i], gf.at[i], gs.at[i], w1p, w2p, act, pre)
+            for kh in range(4):
+                begin(both(partial, i, kh))
+            sweep(1, n_o, lambda k: tokens_out(i, k).start())
+            tokens_out(i, 0).start()
+            if i >= 2:
+                combine(i - 2)
+        for i in range(max(0, ng - 2), ng):
+            combine(i)
+        for i in range(ng):
+            for a in (0, 1):
+                sweep(1, n_s, lambda k: own_w(i, a, k).wait_send())
+                sweep(1, n_s, lambda k: own_t(i, a, k).wait_send())
+                for cs in range(nc):
+                    cross_w(i, a, cs).wait_send()
+                for kh in range(1, 4):
+                    relay_in(i, a, kh).wait_send()
+                relay_out(i, a).wait_send()
+                for kh in range(4):
+                    partial(i, a, kh).wait_send()
+                    for k in range(2 * nc):
+                        if kh or k:
+                            grads_out(i, a, kh, k).wait_send()
+            sweep(1, n_o, lambda k: tokens_out(i, k).wait_send())
+
+    @pl.when(outer)
+    def _():
+        for i in range(ng):
+            for kh in (1, 2, 3, 0):
+                for cs in range(nc):
+                    begin(both(plane_w, i, cs, kh))
+        for i in range(ng):
+            for kh in (1, 2, 3, 0):
+                for cs in range(nc):
+                    begin(both(plane_t, i, cs, kh))
+        for i in range(ng):
+            for a in (0, 1):
+                arrived(WB[a].at[i, :, :, span(0, nc * rows)], wout.at[i, a])
+                begin([up_w(i, a, cs) for cs in range(nc)])
+        for i in range(ng):
+            for a in (0, 1):
+                arrived(XB[a].at[i, :, span(0, nc * tok)], tin.at[i, a])
+                begin([up_t(i, a, cs) for cs in range(nc)])
+        for i in range(ng):
+            for a in (0, 1):
+                for cs in range(nc):
+                    for kh in range(1, 4):
+                        plane_w(i, a, cs, kh).wait_send()
+                        plane_t(i, a, cs, kh).wait_send()
+                    up_w(i, a, cs).wait_send()
+                    up_t(i, a, cs).wait_send()
+
+    arrived(igo, done.at[0])
+    arrived(gfo, done.at[1])
+    arrived(gso, done.at[2])
+
+
+def by_lanes(plan, inputs, cotangent, first_weight, second_weight, orders):
+    tok, width = inputs.shape
+    rows = first_weight.shape[2]
+    nc, ng, bf = plan.nc, plan.ng, jnp.bfloat16
+    scale = 1.0 / math.sqrt(tok * 4 * nc)
+    dma = pltpu.SemaphoreType.DMA
+    toks = pltpu.VMEM((ng, 4, 2 * nc * tok, B), bf)
+    mats = pltpu.VMEM((ng, 4, 2, B, B), bf)
+    half = pltpu.VMEM((ng, 4, 2, 2 * nc * rows, B), bf)
+    part = jax.ShapeDtypeStruct(first_weight.shape, bf)
+    input_grad, first, second = pl.pallas_call(
+        functools.partial(lanes, plan, scale),
+        out_shape=(jax.ShapeDtypeStruct((tok, width), bf), part, part),
+        in_specs=[pl.BlockSpec(memory_space=pltpu.VMEM)] + [ANY] * 4,
+        out_specs=(ANY,) * 3,
+        scratch_shapes=[toks, toks, mats, mats, toks, mats, mats, half, half]
+        + [pltpu.VMEM((4, B, B), bf)] * 2
+        + [pltpu.VMEM((4, 2 * nc * tok, B), bf)] * 2
+        + [dma((ng, 2)), dma((ng, 2, 4)), dma((ng, 2)), dma((ng, 2)), dma((ng, 2, 4)), dma((3,))]
+        + [dma((ng, 2, 4 * nc)), dma((ng, 2, 4 * nc)), dma((ng, 2, nc)), dma((ng, 2, 4)), dma((ng, 2)), dma((ng, 4, nc))]
+        + [dma((ng, 8 * nc)), dma((ng, 2, 4)), dma((ng, 2, 4, 2 * nc))],
+        compiler_params=pltpu.CompilerParams(
+            collective_id=0, has_side_effects=True, vmem_limit_bytes=58 * 2**20
+        ),
+        name="lanes",
+    )(orders, inputs, cotangent, first_weight, second_weight)
+    return input_grad, first.astype(jnp.float32), second.astype(jnp.float32)
 
 
 def dot(left, right, dims=(((1,), (0,)), ((), ()))):
@@ -232,7 +491,11 @@
     out_specs = (P("dp", "mp"), P("mp", None, "dp", None), P("mp", None, "dp", None))
 
     def body(inputs, *rest):
-        plan = Plan(mesh.shape["dp"], mesh.shape["mp"], inputs.shape[1] // B)
+        sizes = mesh.shape["dp"], mesh.shape["mp"], inputs.shape[1] // B
+        plan = Lanes(*sizes)
+        if plan.fits:
+            return by_lanes(plan, inputs, *rest)
+        plan = Plan(*sizes)
         return shards(plan, inputs, *rest)
 
     return jax.shard_map(body, mesh=mesh, in_specs=in_specs, out_specs=out_specs, check_vma=False)

time: 227 us -> 210 us (0.925)
  Pallas kernels: 218 us -> 200 us
    pallas_call x1, Pallas kernels: 218 us -> 200 us  [by_lanes(): pl.pallas_call(functools.partial(lanes, plan, scale), out_shape=(jax.Shap...]
    reduce_sum x1 -> x0, other arithmetic: 5.88 us -> none  [shards(): total = lambda parts: jnp.sum(parts.astype(jnp.float32), axis=0)]
    convert_element_type x0 -> x2, other arithmetic: none -> 4.48 us  [by_lanes(): return (input_grad, first.astype(jnp.float32), second.astype(jnp.float32))]
where the time goes in v1:
time: 210 us; the launch traced here: 207 us
  Pallas kernels  200 us (95%)
  other arithmetic  4.48 us (2%)
    pallas_call x1, Pallas kernels, by_lanes(): pl.pallas_call(functools.partial(lanes, plan, scale), out_shape=(jax.Shap...  200 us
    convert_element_type x2, other arithmetic, by_lanes(): return (input_grad, first.astype(jnp.float32), second.astype(jnp.float32))  4.48 us

profile of v1, /device:TPU:9, one launch (start us, length us, event | category | flops | bytes accessed | tf_op | source)
XLA Modules:
  0.0 207.4 jit_solution(967963593314632589)
XLA Ops:
  0.6 200.2 %lanes.1 = (bf16[128,8192]{1,0:T(8,128)(2,1)}, bf16[32,2,32,256]{3,2,1,0:T(8,128)(2,1)}, bf16[32,2,32,256]{3,2,1,0:T(8,128)(2,1)}) custom-call(s32[2,256]{1,0:T(2,128)} %order.1, bf16[128,8192]{1,0:T(8,128)(2,1)} %x.1, bf16[128,8192]{1,0:T(8,128)(2,1)} %c.1, bf16[32,2,32,256]{3,2,1,0:T(8,128)(2,1)} %w1.1, bf16[32,2,32,256]{3,2,1,0:T(8,128)(2,1)} %w2.1), custom_call_target="tpu_custom_call" | custom-call | tf_op jit(solution)/shard_map/lanes/pallas_call | solution.py:399
  200.8 0.0 copy-start.1
  200.8 2.9 %convert_element_type.6 = f32[32,2,32,256]{3,2,1,0:T(8,128)} convert(bf16[32,2,32,256]{3,2,1,0:T(8,128)(2,1)} %get-tuple-element.7) | non-fusion elementwise | flops 524288 | bytes 3145728 | tf_op jit(solution)/shard_map/convert_element_type | solution.py:415
  203.7 0.0 copy-done.1
  203.7 0.0 copy-start
  203.7 1.6 convert_element_type.7
  205.3 0.8 copy-done
  206.1 1.3 copy.9
Async XLA Ops:
  200.8 2.9 %copy-start.1 = (bf16[32,2,32,256]{3,2,1,0:T(8,128)(2,1)S(1)}, bf16[32,2,32,256]{3,2,1,0:T(8,128)(2,1)}, u32[]{:S(2)}) copy-start(bf16[32,2,32,256]{3,2,1,0:T(8,128)(2,1)} %get-tuple-element.8) | copy-start | bytes 3145732
  203.7 2.3 %copy-start = (bf16[128,8192]{1,0:T(8,128)(2,1)S(1)}, bf16[128,8192]{1,0:T(8,128)(2,1)}, u32[]{:S(2)}) copy-start(bf16[128,8192]{1,0:T(8,128)(2,1)} %get-tuple-element.12) | copy-start | bytes 6291460

commit v2 on v1

--- a/solution.py
+++ b/solution.py
@@ -275,17 +275,19 @@
             return pltpu.make_async_copy(s, e, done.at[0])
         return put(s, e, si.at[i, k], done.at[0], (first + u // 4, mp_of(u % 4)))
 
-    def partial(i, a, kh):
-        hh = (h + kh) % 4
-        s = G[a].at[i, hh, :, span(1 - side, 2 * nc * rows)]
-        return put(s, GI[a].at[i, hh], sg.at[i, a, kh], gin.at[i, a, kh], (other + core, m))
-
-    def grads_out(i, a, kh, k):
-        hh, r = (h + kh) % 4, (slot + k) % (2 * nc)
-        s, e = GI[a].at[i, hh, :, span(r, rows)], GO[a].at[me * ng + i]
-        if kh == 0 and k == 0:
+    def partial(i, a, kh, near):
+        hh, theirs = (h + kh) % 4, other // nc if near else 3 - far // nc
+        s = G[a].at[i, hh, :, span(theirs, nc * rows)]
+        return put(s, GI[a].at[i, hh, near], sg.at[i, a, kh, near], gin.at[i, a, kh, near], (other + core, m))
+
+    def grads_out(i, a, kh, near, k):
+        hh, cs = (h + kh) % 4, (core + k) % nc
+        s, e = GI[a].at[i, hh, near, :, span(cs, rows)], GO[a].at[me * ng + i]
+        if near and kh == 0 and k == 0:
             return pltpu.make_async_copy(s, e, done.at[1 + a])
-        return put(s, e, sf.at[i, a, kh, k], done.at[1 + a], (first + r, mp_of(hh)))
+        return put(s, e, sf.at[i, a, kh, near, k], done.at[1 + a], ((base if near else far) + cs, mp_of(hh)))
+
+    parts = [(a, kh, near) for near in (0, 1) for kh in (1, 2, 3, 0) for a in (0, 1)]
 
     def both(f, *at):
         return [f(at[0], a, *at[1:]) for a in (0, 1)]
@@ -295,13 +297,13 @@
             copy.start()
 
     def combine(i):
-        for kh in range(4):
+        for a, kh, near in parts:
             hh = (h + kh) % 4
-            for a in (0, 1):
-                arrived(GI[a].at[i, hh], gin.at[i, a, kh])
-                mine = G[a][i, hh, :, span(side, 2 * nc * rows)].astype(jnp.float32)
-                GI[a][i, hh] = (mine + GI[a][i, hh].astype(jnp.float32)).astype(jnp.bfloat16)
-                begin([grads_out(i, a, kh, k) for k in range(2 * nc)])
+            arrived(GI[a].at[i, hh, near], gin.at[i, a, kh, near])
+            ours = base // nc if near else far // nc
+            mine = G[a][i, hh, :, span(ours, nc * rows)].astype(jnp.float32)
+            GI[a][i, hh, near] = (mine + GI[a][i, hh, near].astype(jnp.float32)).astype(jnp.bfloat16)
+            begin([grads_out(i, a, kh, near, k) for k in range(nc)])
 
     @pl.when(inner)
     def _():
@@ -330,14 +332,12 @@
                 arrived(WB[a].at[i, :, :, span(1 - side, 2 * nc * rows)], wrel.at[i, a])
                 arrived(XB[a].at[i], tin.at[i, a])
             factors(scale, order, xb.at[i], cb.at[i], w1b.at[i], w2b.at[i], ig.at[i], gf.at[i], gs.at[i], w1p, w2p, act, pre)
-            for kh in range(4):
-                begin(both(partial, i, kh))
+            begin([partial(i, *at) for at in parts])
             sweep(1, n_o, lambda k: tokens_out(i, k).start())
             tokens_out(i, 0).start()
-            if i >= 2:
-                combine(i - 2)
-        for i in range(max(0, ng - 2), ng):
-            combine(i)
+            if i >= 1:
+                combine(i - 1)
+        combine(ng - 1)
         for i in range(ng):
             for a in (0, 1):
                 sweep(1, n_s, lambda k: own_w(i, a, k).wait_send())
@@ -347,12 +347,12 @@
                 for kh in range(1, 4):
                     relay_in(i, a, kh).wait_send()
                 relay_out(i, a).wait_send()
-                for kh in range(4):
-                    partial(i, a, kh).wait_send()
-                    for k in range(2 * nc):
-                        if kh or k:
-                            grads_out(i, a, kh, k).wait_send()
             sweep(1, n_o, lambda k: tokens_out(i, k).wait_send())
+            for a, kh, near in parts:
+                partial(i, a, kh, near).wait_send()
+                for k in range(nc):
+                    if not near or kh or k:
+                        grads_out(i, a, kh, near, k).wait_send()
 
     @pl.when(outer)
     def _():
@@ -394,7 +394,7 @@
     dma = pltpu.SemaphoreType.DMA
     toks = pltpu.VMEM((ng, 4, 2 * nc * tok, B), bf)
     mats = pltpu.VMEM((ng, 4, 2, B, B), bf)
-    half = pltpu.VMEM((ng, 4, 2, 2 * nc * rows, B), bf)
+    half = pltpu.VMEM((ng, 4, 2, 2, nc * rows, B), bf)
     part = jax.ShapeDtypeStruct(first_weight.shape, bf)
     input_grad, first, second = pl.pallas_call(
         functools.partial(lanes, plan, scale),
@@ -404,9 +404,9 @@
         scratch_shapes=[toks, toks, mats, mats, toks, mats, mats, half, half]
         + [pltpu.VMEM((4, B, B), bf)] * 2
         + [pltpu.VMEM((4, 2 * nc * tok, B), bf)] * 2
-        + [dma((ng, 2)), dma((ng, 2, 4)), dma((ng, 2)), dma((ng, 2)), dma((ng, 2, 4)), dma((3,))]
+        + [dma((ng, 2)), dma((ng, 2, 4)), dma((ng, 2)), dma((ng, 2)), dma((ng, 2, 4, 2)), dma((3,))]
         + [dma((ng, 2, 4 * nc)), dma((ng, 2, 4 * nc)), dma((ng, 2, nc)), dma((ng, 2, 4)), dma((ng, 2)), dma((ng, 4, nc))]
-        + [dma((ng, 8 * nc)), dma((ng, 2, 4)), dma((ng, 2, 4, 2 * nc))],
+        + [dma((ng, 8 * nc)), dma((ng, 2, 4, 2)), dma((ng, 2, 4, 2, nc))],
         compiler_params=pltpu.CompilerParams(
             collective_id=0, has_side_effects=True, vmem_limit_bytes=58 * 2**20
         ),

time: 210 us -> 201 us (0.957); the launches traced: 207 us -> 201 us
  Pallas kernels: 200 us -> 194 us
    pallas_call x1, Pallas kernels: 200 us -> 194 us  [by_lanes(): pl.pallas_call(functools.partial(lanes, plan, scale), out_shape=(jax.Shap...]
where the time goes in v2:
time: 201 us
  Pallas kernels  194 us (97%)
  other arithmetic  4.48 us (2%)
  local copies, waits for them, and re-layouts  2.09 us (1%)
    pallas_call x1, Pallas kernels, by_lanes(): pl.pallas_call(functools.partial(lanes, plan, scale), out_shape=(jax.Shap...  194 us
    convert_element_type x2, other arithmetic, by_lanes(): return (input_grad, first.astype(jnp.float32), second.astype(jnp.float32))  4.48 us

profile of v2, /device:TPU:9, one launch (start us, length us, event | category | flops | bytes accessed | tf_op | source)
XLA Modules:
  0.0 200.7 jit_solution(2401897115235052335)
XLA Ops:
  0.6 193.5 %lanes.1 = (bf16[128,8192]{1,0:T(8,128)(2,1)}, bf16[32,2,32,256]{3,2,1,0:T(8,128)(2,1)}, bf16[32,2,32,256]{3,2,1,0:T(8,128)(2,1)}) custom-call(s32[2,256]{1,0:T(2,128)} %order.1, bf16[128,8192]{1,0:T(8,128)(2,1)} %x.1, bf16[128,8192]{1,0:T(8,128)(2,1)} %c.1, bf16[32,2,32,256]{3,2,1,0:T(8,128)(2,1)} %w1.1, bf16[32,2,32,256]{3,2,1,0:T(8,128)(2,1)} %w2.1), custom_call_target="tpu_custom_call" | custom-call | tf_op jit(solution)/shard_map/lanes/pallas_call | solution.py:399
  194.2 0.0 copy-start.1
  194.2 2.9 %convert_element_type.6 = f32[32,2,32,256]{3,2,1,0:T(8,128)} convert(bf16[32,2,32,256]{3,2,1,0:T(8,128)(2,1)} %get-tuple-element.7) | non-fusion elementwise | flops 524288 | bytes 3145728 | tf_op jit(solution)/shard_map/convert_element_type | solution.py:415
  197.1 0.0 copy-done.1
  197.1 0.0 copy-start
  197.1 1.6 convert_element_type.7
  198.7 0.8 copy-done
  199.4 1.3 copy.9
Async XLA Ops:
  194.2 2.9 %copy-start.1 = (bf16[32,2,32,256]{3,2,1,0:T(8,128)(2,1)S(1)}, bf16[32,2,32,256]{3,2,1,0:T(8,128)(2,1)}, u32[]{:S(2)}) copy-start(bf16[32,2,32,256]{3,2,1,0:T(8,128)(2,1)} %get-tuple-element.8) | copy-start | bytes 3145732
  197.1 2.3 %copy-start = (bf16[128,8192]{1,0:T(8,128)(2,1)S(1)}, bf16[128,8192]{1,0:T(8,128)(2,1)}, u32[]{:S(2)}) copy-start(bf16[128,8192]{1,0:T(8,128)(2,1)} %get-tuple-element.12) | copy-start | bytes 6291460

commit v3 on v2

--- a/solution.py
+++ b/solution.py
@@ -164,7 +164,7 @@
         self.fits = dp % 4 == 0 and mp % 4 == 0 and self.ng > 0 and local_blocks % (4 * nc) == 0
 
 
-def lanes(plan, scale, order, x, c, w1, w2, igo, gfo, gso, xb, cb, w1b, w2b, ig, gf, gs, gif, gis, w1p, w2p, act, pre,
+def lanes(plan, scale, orders, x, c, w1, w2, igo, gfo, gso, order, ordered, xb, cb, w1b, w2b, ig, gf, gs, gif, gis, w1p, w2p, act, pre,
           tin, win, wout, wrel, gin, done, st, sw, sd, sr, so, su, si, sg, sf):
     nc, low, ng = plan.nc, plan.low, plan.ng
     tok, rows = x.shape[0], w1.shape[2]
@@ -310,6 +310,7 @@
         for i in range(ng):
             for cs in range(nc):
                 begin(both(cross_w, i, cs))
+        pltpu.make_async_copy(orders, order, ordered).start()
         for i in range(ng):
             sweep(1, n_s, lambda k: begin(both(own_w, i, k)))
             begin(both(own_w, i, 0))
@@ -327,6 +328,7 @@
             for a in (0, 1):
                 arrived(WB[a].at[i, :, :, span(far // nc, nc * rows)], wout.at[i, a])
                 relay_out(i, a).start()
+        arrived(order, ordered)
         for i in range(ng):
             for a in (0, 1):
                 arrived(WB[a].at[i, :, :, span(1 - side, 2 * nc * rows)], wrel.at[i, a])
@@ -395,13 +397,14 @@
     toks = pltpu.VMEM((ng, 4, 2 * nc * tok, B), bf)
     mats = pltpu.VMEM((ng, 4, 2, B, B), bf)
     half = pltpu.VMEM((ng, 4, 2, 2, nc * rows, B), bf)
-    part = jax.ShapeDtypeStruct(first_weight.shape, bf)
+    part = pltpu.VMEM(first_weight.shape, bf)
     input_grad, first, second = pl.pallas_call(
         functools.partial(lanes, plan, scale),
-        out_shape=(jax.ShapeDtypeStruct((tok, width), bf), part, part),
-        in_specs=[pl.BlockSpec(memory_space=pltpu.VMEM)] + [ANY] * 4,
+        out_shape=(pltpu.VMEM((tok, width), bf), part, part),
+        in_specs=[ANY] * 5,
         out_specs=(ANY,) * 3,
-        scratch_shapes=[toks, toks, mats, mats, toks, mats, mats, half, half]
+        scratch_shapes=[pltpu.VMEM(orders.shape, orders.dtype), dma]
+        + [toks, toks, mats, mats, toks, mats, mats, half, half]
         + [pltpu.VMEM((4, B, B), bf)] * 2
         + [pltpu.VMEM((4, 2 * nc * tok, B), bf)] * 2
         + [dma((ng, 2)), dma((ng, 2, 4)), dma((ng, 2)), dma((ng, 2)), dma((ng, 2, 4, 2)), dma((3,))]

time: 201 us -> 199 us (0.990)
  no operation moved by 1% of the time
where the time goes in v3:
time: 199 us; the launch traced here: 198 us
  Pallas kernels  193 us (97%)
  other arithmetic  3.17 us (2%)
    pallas_call x1, Pallas kernels, by_lanes(): pl.pallas_call(functools.partial(lanes, plan, scale), out_shape=(pltpu.VM...  193 us

profile of v3, /device:TPU:9, one launch (start us, length us, event | category | flops | bytes accessed | tf_op | source)
XLA Modules:
  0.0 198.2 jit_solution(2049660504721005913)
XLA Ops:
  0.6 193.0 %lanes.1 = (bf16[128,8192]{1,0:T(8,128)(2,1)S(1)}, bf16[32,2,32,256]{3,2,1,0:T(8,128)(2,1)S(1)}, bf16[32,2,32,256]{3,2,1,0:T(8,128)(2,1)S(1)}) custom-call(s32[2,256]{1,0:T(2,128)} %orders.1, bf16[128,8192]{1,0:T(8,128)(2,1)} %x.1, bf16[128,8192]{1,0:T(8,128)(2,1)} %c.1, bf16[32,2,32,256]{3,2,1,0:T(8,128)(2,1)} %w1.1, bf16[32,2,32,256]{3,2,1,0:T(8,128)(2,1)} %w2.1), custom_call_target="tpu_custom_call" | custom-call | tf_op jit(solution)/shard_map/lanes/pallas_call | solution.py:401
  193.7 1.3 copy.9
  195.0 1.6 convert_element_type.6
  196.6 1.6 convert_element_type.7

commit v4 on v3

--- a/solution.py
+++ b/solution.py
@@ -9,6 +9,7 @@
 from jax.sharding import PartitionSpec as P
 
 B = 256
+CHUNKS = 4
 MESH = pl.DeviceIdType.MESH
 ANY = pl.BlockSpec(memory_space=pl.ANY)
 NT = (((1,), (1,)), ((), ()))
@@ -198,21 +199,20 @@
 
     @pl.when(inner)
     def _():
-        for k in range(1, n_o):
-            u = (us + k) % n_o
-            hello((first + u // 4, mp_of(u % 4)))
         for cs in range(nc):
             hello((other + cs, m))
-        pl.semaphore_wait(barrier, n_o - 1 + nc)
+        for k in range(1, n_s):
+            t = (me + k) % n_s
+            hello((base + t // 4, mp_of(t % 4)))
+        for cs in range(nc):
+            hello((far + cs, m))
+        pl.semaphore_wait(barrier, n_s - 1 + nc)
 
     @pl.when(outer)
     def _():
-        for k in range(n_s):
-            t = (me + k) % n_s
-            hello((base + t // 4, mp_of(t % 4)))
         for kh in range(1, 4):
             hello((d, mp_of((h + kh) % 4)))
-        pl.semaphore_wait(barrier, n_s + 3)
+        pl.semaphore_wait(barrier, nc + 3)
 
     def block_of(a, t, i):
         return W[a].at[t * ng + i]
@@ -415,7 +415,34 @@
         ),
         name="lanes",
     )(orders, inputs, cotangent, first_weight, second_weight)
-    return input_grad, first.astype(jnp.float32), second.astype(jnp.float32)
+    return finish(input_grad, first, second)
+
+
+def store(ig, first, second, igo, fo, so, fw, sw, sems):
+    copies = [pltpu.make_async_copy(ig, igo, sems.at[0, 0])]
+    copies[0].start()
+    size = max(1, first.shape[0] // CHUNKS)
+    for n, at in enumerate(range(0, first.shape[0], size)):
+        for a, (src, wide, dst) in enumerate(((first, fw, fo), (second, sw, so))):
+            rows = pl.ds(at, size)
+            wide[rows] = src[rows].astype(jnp.float32)
+            copies.append(pltpu.make_async_copy(wide.at[rows], dst.at[rows], sems.at[1 + a, n]))
+            copies[-1].start()
+    for copy in copies:
+        copy.wait()
+
+
+def finish(input_grad, first, second):
+    wide = jax.ShapeDtypeStruct(first.shape, jnp.float32)
+    return pl.pallas_call(
+        store,
+        out_shape=(jax.ShapeDtypeStruct(input_grad.shape, input_grad.dtype), wide, wide),
+        in_specs=[pl.BlockSpec(memory_space=pltpu.VMEM)] * 3,
+        out_specs=(ANY,) * 3,
+        scratch_shapes=[pltpu.VMEM(first.shape, jnp.float32)] * 2 + [pltpu.SemaphoreType.DMA((3, CHUNKS))],
+        compiler_params=pltpu.CompilerParams(vmem_limit_bytes=48 * 2**20),
+        name="store",
+    )(input_grad, first, second)
 
 
 def dot(left, right, dims=(((1,), (0,)), ((), ()))):

time: 199 us -> 196 us (0.985)
  other arithmetic: 3.17 us -> 0 us
  Pallas kernels: 193 us -> 195 us
    convert_element_type x2 -> x0, other arithmetic: 3.17 us -> none  [by_lanes(): return (input_grad, first.astype(jnp.float32), second.astype(jnp.float32))]
    pallas_call x0 -> x1, Pallas kernels: none -> 2.75 us  [finish(): pl.pallas_call(store, out_shape=(jax.ShapeDtypeStruct(input_grad.shape, i...]
where the time goes in v4:
time: 196 us; the launch traced here: 195 us
  Pallas kernels  195 us (99%)
    pallas_call x1, Pallas kernels, by_lanes(): pl.pallas_call(functools.partial(lanes, plan, scale), out_shape=(pltpu.VM...  192 us

profile of v4, /device:TPU:9, one launch (start us, length us, event | category | flops | bytes accessed | tf_op | source)
XLA Modules:
  0.0 195.4 jit_solution(4375782117533210015)
XLA Ops:
  0.6 191.8 %lanes.1 = (bf16[128,8192]{1,0:T(8,128)(2,1)S(1)}, bf16[32,2,32,256]{3,2,1,0:T(8,128)(2,1)S(1)}, bf16[32,2,32,256]{3,2,1,0:T(8,128)(2,1)S(1)}) custom-call(s32[2,256]{1,0:T(2,128)} %orders.1, bf16[128,8192]{1,0:T(8,128)(2,1)} %x.1, bf16[128,8192]{1,0:T(8,128)(2,1)} %c.1, bf16[32,2,32,256]{3,2,1,0:T(8,128)(2,1)} %w1.1, bf16[32,2,32,256]{3,2,1,0:T(8,128)(2,1)} %w2.1), custom_call_target="tpu_custom_call" | custom-call | tf_op jit(solution)/shard_map/lanes/pallas_call | solution.py:401
  192.4 2.8 %store.1 = (bf16[128,8192]{1,0:T(8,128)(2,1)}, f32[32,2,32,256]{3,2,1,0:T(8,128)}, f32[32,2,32,256]{3,2,1,0:T(8,128)}) custom-call(bf16[128,8192]{1,0:T(8,128)(2,1)S(1)} %get-tuple-element.6.ig, bf16[32,2,32,256]{3,2,1,0:T(8,128)(2,1)S(1)} %get-tuple-element.7.first, bf16[32,2,32,256]{3,2,1,0:T(8,128)(2,1)S(1)} %get-tuple-element.8.second), custom_call_target="tpu_custom_call" | custom-call | tf_op jit(solution)/shard_map/store/pallas_call | solution.py:437

commit v5 on v4

--- a/solution.py
+++ b/solution.py
@@ -166,7 +166,7 @@
 
 
 def lanes(plan, scale, orders, x, c, w1, w2, igo, gfo, gso, order, ordered, xb, cb, w1b, w2b, ig, gf, gs, gif, gis, w1p, w2p, act, pre,
-          tin, win, wout, wrel, gin, done, st, sw, sd, sr, so, su, si, sg, sf):
+          tin, win, wout, wrel, gin, done, st, sw, sr, si, sg, sf):
     nc, low, ng = plan.nc, plan.low, plan.ng
     tok, rows = x.shape[0], w1.shape[2]
     d, m = lax.axis_index("dp"), lax.axis_index("mp")
@@ -225,67 +225,67 @@
         e = WB[a].at[i, h, :, span(d, rows)]
         if isinstance(k, int) and k == 0:
             return pltpu.make_async_copy(block_of(a, t, i), e, win.at[i, a, h])
-        return put(block_of(a, t, i), e, sw.at[i, a, k], win.at[i, a, h], (base + t // 4, mp_of(t % 4)))
+        return put(block_of(a, t, i), e, sw.at[0, a], win.at[i, a, h], (base + t // 4, mp_of(t % 4)))
 
     def cross_w(i, a, cs):
         e = WB[a].at[i, h, :, span(d, rows)]
-        return put(block_of(a, cs * 4 + h, i), e, sd.at[i, a, cs], wrel.at[i, a], (other + cs, m))
+        return put(block_of(a, cs * 4 + h, i), e, sw.at[1, a], wrel.at[i, a], (other + cs, m))
 
     def own_t(i, a, k):
         t = (me + k) % n_s
         e = XB[a].at[i, h, span(slot, tok)]
         if isinstance(k, int) and k == 0:
             return pltpu.make_async_copy(columns_of(a, t, i), e, tin.at[i, a])
-        return put(columns_of(a, t, i), e, st.at[i, a, k], tin.at[i, a], (base + t // 4, mp_of(t % 4)))
+        return put(columns_of(a, t, i), e, st.at[0, a], tin.at[i, a], (base + t // 4, mp_of(t % 4)))
 
     def plane_w(i, a, cs, kh):
         hh = (h + kh) % 4
         s, e = block_of(a, cs * 4 + hh, i), WB[a].at[i, h, :, span(cs, rows)]
         if kh == 0:
             return pltpu.make_async_copy(s, e, wout.at[i, a])
-        return put(s, e, sw.at[i, a, cs * 4 + kh], wout.at[i, a], (d, mp_of(hh)))
+        return put(s, e, sw.at[0, a], wout.at[i, a], (d, mp_of(hh)))
 
     def plane_t(i, a, cs, kh):
         hh = (h + kh) % 4
         s, e = columns_of(a, cs * 4 + hh, i), XB[a].at[i, h, span(cs, tok)]
         if kh == 0:
             return pltpu.make_async_copy(s, e, tin.at[i, a])
-        return put(s, e, st.at[i, a, cs * 4 + kh], tin.at[i, a], (d, mp_of(hh)))
+        return put(s, e, st.at[0, a], tin.at[i, a], (d, mp_of(hh)))
 
     def up_w(i, a, cs):
         s, e = WB[a].at[i, :, :, span(cs, rows)], WB[a].at[i, :, :, span(d, rows)]
-        return put(s, e, su.at[i, a, cs], wout.at[i, a], (base + cs, m))
+        return put(s, e, sw.at[1, a], wout.at[i, a], (base + cs, m))
 
     def up_t(i, a, cs):
         s, e = XB[a].at[i, :, span(cs, tok)], XB[a].at[i, :, span(slot, tok)]
-        return put(s, e, su.at[i, 2 + a, cs], tin.at[i, a], (base + cs, m))
+        return put(s, e, st.at[1, a], tin.at[i, a], (base + cs, m))
 
     def relay_in(i, a, kh):
         s = WB[a].at[i, (h + kh) % 4, :, span(base // nc, nc * rows)]
-        return put(s, s, sr.at[i, a, kh], wrel.at[i, a], (other + core, m))
+        return put(s, s, sr.at[0, a], wrel.at[i, a], (other + core, m))
 
     def relay_out(i, a):
         s = WB[a].at[i, :, :, span(far // nc, nc * rows)]
-        return put(s, s, so.at[i, a], wrel.at[i, a], (other + core, m))
-
-    def tokens_out(i, k):
+        return put(s, s, sr.at[1, a], wrel.at[i, a], (other + core, m))
+
+    def tokens_out(i, k, more=0):
         u = (us + k) % n_o
         s, e = ig.at[i, u % 4, span(u // 4, tok)], igo.at[:, span(me * ng + i, B)]
         if isinstance(k, int) and k == 0:
             return pltpu.make_async_copy(s, e, done.at[0])
-        return put(s, e, si.at[i, k], done.at[0], (first + u // 4, mp_of(u % 4)))
+        return put(s, e, si.at[more], done.at[0], (first + u // 4, mp_of(u % 4)))
 
     def partial(i, a, kh, near):
         hh, theirs = (h + kh) % 4, other // nc if near else 3 - far // nc
         s = G[a].at[i, hh, :, span(theirs, nc * rows)]
-        return put(s, GI[a].at[i, hh, near], sg.at[i, a, kh, near], gin.at[i, a, kh, near], (other + core, m))
+        return put(s, GI[a].at[i, hh, near], sg.at[a], gin.at[i, a, kh, near], (other + core, m))
 
     def grads_out(i, a, kh, near, k):
         hh, cs = (h + kh) % 4, (core + k) % nc
         s, e = GI[a].at[i, hh, near, :, span(cs, rows)], GO[a].at[me * ng + i]
         if near and kh == 0 and k == 0:
             return pltpu.make_async_copy(s, e, done.at[1 + a])
-        return put(s, e, sf.at[i, a, kh, near, k], done.at[1 + a], ((base if near else far) + cs, mp_of(hh)))
+        return put(s, e, sf.at[near, a], done.at[1 + a], ((base if near else far) + cs, mp_of(hh)))
 
     parts = [(a, kh, near) for near in (0, 1) for kh in (1, 2, 3, 0) for a in (0, 1)]
 
@@ -335,26 +335,24 @@
                 arrived(XB[a].at[i], tin.at[i, a])
             factors(scale, order, xb.at[i], cb.at[i], w1b.at[i], w2b.at[i], ig.at[i], gf.at[i], gs.at[i], w1p, w2p, act, pre)
             begin([partial(i, *at) for at in parts])
-            sweep(1, n_o, lambda k: tokens_out(i, k).start())
+            sweep(1, n_s, lambda k: tokens_out(i, k).start())
+            sweep(n_s, n_o, lambda k: tokens_out(i, k, 1).start())
             tokens_out(i, 0).start()
             if i >= 1:
                 combine(i - 1)
         combine(ng - 1)
-        for i in range(ng):
-            for a in (0, 1):
-                sweep(1, n_s, lambda k: own_w(i, a, k).wait_send())
-                sweep(1, n_s, lambda k: own_t(i, a, k).wait_send())
-                for cs in range(nc):
-                    cross_w(i, a, cs).wait_send()
-                for kh in range(1, 4):
-                    relay_in(i, a, kh).wait_send()
-                relay_out(i, a).wait_send()
-            sweep(1, n_o, lambda k: tokens_out(i, k).wait_send())
-            for a, kh, near in parts:
-                partial(i, a, kh, near).wait_send()
-                for k in range(nc):
-                    if not near or kh or k:
-                        grads_out(i, a, kh, near, k).wait_send()
+        some = ng * (n_s - 1)
+        arrived(igo.at[:, pl.ds(0, some * B)], si.at[0])
+        arrived(igo, si.at[1])
+        for a in (0, 1):
+            arrived(X[a].at[:, pl.ds(0, some * B)], st.at[0, a])
+            arrived(W[a].at[pl.ds(0, some)], sw.at[0, a])
+            arrived(W[a].at[pl.ds(0, ng * nc)], sw.at[1, a])
+            arrived(WB[a].at[:, pl.ds(0, 3), :, pl.ds(0, nc * rows)], sr.at[0, a])
+            arrived(WB[a].at[:, :, :, pl.ds(0, nc * rows)], sr.at[1, a])
+            arrived(GI[a], sg.at[a])
+            arrived(GO[a], sf.at[0, a])
+            arrived(GO[a].at[pl.ds(0, some)], sf.at[1, a])
 
     @pl.when(outer)
     def _():
@@ -374,14 +372,11 @@
             for a in (0, 1):
                 arrived(XB[a].at[i, :, span(0, nc * tok)], tin.at[i, a])
                 begin([up_t(i, a, cs) for cs in range(nc)])
-        for i in range(ng):
-            for a in (0, 1):
-                for cs in range(nc):
-                    for kh in range(1, 4):
-                        plane_w(i, a, cs, kh).wait_send()
-                        plane_t(i, a, cs, kh).wait_send()
-                    up_w(i, a, cs).wait_send()
-                    up_t(i, a, cs).wait_send()
+        for a in (0, 1):
+            arrived(W[a].at[pl.ds(0, 3 * ng * nc)], sw.at[0, a])
+            arrived(X[a].at[:, pl.ds(0, 3 * ng * nc * B)], st.at[0, a])
+            arrived(W[a], sw.at[1, a])
+            arrived(X[a], st.at[1, a])
 
     arrived(igo, done.at[0])
     arrived(gfo, done.at[1])
@@ -408,8 +403,7 @@
         + [pltpu.VMEM((4, B, B), bf)] * 2
         + [pltpu.VMEM((4, 2 * nc * tok, B), bf)] * 2
         + [dma((ng, 2)), dma((ng, 2, 4)), dma((ng, 2)), dma((ng, 2)), dma((ng, 2, 4, 2)), dma((3,))]
-        + [dma((ng, 2, 4 * nc)), dma((ng, 2, 4 * nc)), dma((ng, 2, nc)), dma((ng, 2, 4)), dma((ng, 2)), dma((ng, 4, nc))]
-        + [dma((ng, 8 * nc)), dma((ng, 2, 4, 2)), dma((ng, 2, 4, 2, nc))],
+        + [dma((2, 2))] * 3 + [dma((2,))] * 2 + [dma((2, 2))],
         compiler_params=pltpu.CompilerParams(
             collective_id=0, has_side_effects=True, vmem_limit_bytes=58 * 2**20
         ),

time: 196 us -> 191 us (0.974)
  Pallas kernels: 195 us -> 190 us
    pallas_call x1, Pallas kernels: 192 us -> 188 us  [by_lanes(): pl.pallas_call(functools.partial(lanes, plan, scale), out_shape=(pltpu.VM...]
where the time goes in v5:
time: 191 us
  Pallas kernels  190 us (99%)
    pallas_call x1, Pallas kernels, by_lanes(): pl.pallas_call(functools.partial(lanes, plan, scale), out_shape=(pltpu.VM...  188 us

profile of v5, /device:TPU:9, one launch (start us, length us, event | category | flops | bytes accessed | tf_op | source)
XLA Modules:
  0.0 191.3 jit_solution(3859794809975000860)
XLA Ops:
  0.6 187.7 %lanes.1 = (bf16[128,8192]{1,0:T(8,128)(2,1)S(1)}, bf16[32,2,32,256]{3,2,1,0:T(8,128)(2,1)S(1)}, bf16[32,2,32,256]{3,2,1,0:T(8,128)(2,1)S(1)}) custom-call(s32[2,256]{1,0:T(2,128)} %orders.1, bf16[128,8192]{1,0:T(8,128)(2,1)} %x.1, bf16[128,8192]{1,0:T(8,128)(2,1)} %c.1, bf16[32,2,32,256]{3,2,1,0:T(8,128)(2,1)} %w1.1, bf16[32,2,32,256]{3,2,1,0:T(8,128)(2,1)} %w2.1), custom_call_target="tpu_custom_call" | custom-call | tf_op jit(solution)/shard_map/lanes/pallas_call | solution.py:396
  188.4 2.8 %store.1 = (bf16[128,8192]{1,0:T(8,128)(2,1)}, f32[32,2,32,256]{3,2,1,0:T(8,128)}, f32[32,2,32,256]{3,2,1,0:T(8,128)}) custom-call(bf16[128,8192]{1,0:T(8,128)(2,1)S(1)} %get-tuple-element.6.ig, bf16[32,2,32,256]{3,2,1,0:T(8,128)(2,1)S(1)} %get-tuple-element.7.first, bf16[32,2,32,256]{3,2,1,0:T(8,128)(2,1)S(1)} %get-tuple-element.8.second), custom_call_target="tpu_custom_call" | custom-call | tf_op jit(solution)/shard_map/store/pallas_call | solution.py:431

commit v6 on v5

--- a/solution.py
+++ b/solution.py
@@ -165,7 +165,7 @@
         self.fits = dp % 4 == 0 and mp % 4 == 0 and self.ng > 0 and local_blocks % (4 * nc) == 0
 
 
-def lanes(plan, scale, orders, x, c, w1, w2, igo, gfo, gso, order, ordered, xb, cb, w1b, w2b, ig, gf, gs, gif, gis, w1p, w2p, act, pre,
+def lanes(plan, scale, orders, x, c, w1, w2, igo, go, order, ordered, xc, wb, ig, g, gi, w1p, w2p, act, pre,
           tin, win, wout, wrel, gin, done, st, sw, sr, si, sg, sf):
     nc, low, ng = plan.nc, plan.low, plan.ng
     tok, rows = x.shape[0], w1.shape[2]
@@ -177,8 +177,7 @@
     base, other, far = nc + side * nc, 2 * nc - side * nc, 3 * nc * side
     first, me, us = 2 * nc * side, core * 4 + h, slot * 4 + h
     n_s, n_o = 4 * nc, 8 * nc
-    X, W, G, GI, GO = (x, c), (w1, w2), (gf, gs), (gif, gis), (gfo, gso)
-    XB, WB = (xb, cb), (w1b, w2b)
+    X, W = (x, c), (w1, w2)
 
     def mp_of(hh):
         return hh * low + lo
@@ -222,51 +221,51 @@
 
     def own_w(i, a, k):
         t = (me + k) % n_s
-        e = WB[a].at[i, h, :, span(d, rows)]
-        if isinstance(k, int) and k == 0:
-            return pltpu.make_async_copy(block_of(a, t, i), e, win.at[i, a, h])
-        return put(block_of(a, t, i), e, sw.at[0, a], win.at[i, a, h], (base + t // 4, mp_of(t % 4)))
+        e, arrival = wb.at[i, h, pl.ds(2 * a, 2), span(d, rows)], win.at[3 + i if i else h]
+        if isinstance(k, int) and k == 0:
+            return pltpu.make_async_copy(block_of(a, t, i), e, arrival)
+        return put(block_of(a, t, i), e, sw.at[0, a], arrival, (base + t // 4, mp_of(t % 4)))
 
     def cross_w(i, a, cs):
-        e = WB[a].at[i, h, :, span(d, rows)]
-        return put(block_of(a, cs * 4 + h, i), e, sw.at[1, a], wrel.at[i, a], (other + cs, m))
+        e = wb.at[i, h, pl.ds(2 * a, 2), span(d, rows)]
+        return put(block_of(a, cs * 4 + h, i), e, sw.at[1, a], wrel.at[i], (other + cs, m))
 
     def own_t(i, a, k):
         t = (me + k) % n_s
-        e = XB[a].at[i, h, span(slot, tok)]
-        if isinstance(k, int) and k == 0:
-            return pltpu.make_async_copy(columns_of(a, t, i), e, tin.at[i, a])
-        return put(columns_of(a, t, i), e, st.at[0, a], tin.at[i, a], (base + t // 4, mp_of(t % 4)))
+        e = xc.at[i, a, h, span(slot, tok)]
+        if isinstance(k, int) and k == 0:
+            return pltpu.make_async_copy(columns_of(a, t, i), e, tin.at[i])
+        return put(columns_of(a, t, i), e, st.at[a], tin.at[i], (base + t // 4, mp_of(t % 4)))
 
     def plane_w(i, a, cs, kh):
         hh = (h + kh) % 4
-        s, e = block_of(a, cs * 4 + hh, i), WB[a].at[i, h, :, span(cs, rows)]
+        s, e = block_of(a, cs * 4 + hh, i), wb.at[i, h, pl.ds(2 * a, 2), span(cs, rows)]
         if kh == 0:
-            return pltpu.make_async_copy(s, e, wout.at[i, a])
-        return put(s, e, sw.at[0, a], wout.at[i, a], (d, mp_of(hh)))
+            return pltpu.make_async_copy(s, e, wout.at[i])
+        return put(s, e, sw.at[0, a], wout.at[i], (d, mp_of(hh)))
 
     def plane_t(i, a, cs, kh):
         hh = (h + kh) % 4
-        s, e = columns_of(a, cs * 4 + hh, i), XB[a].at[i, h, span(cs, tok)]
+        s, e = columns_of(a, cs * 4 + hh, i), xc.at[i, a, h, span(cs, tok)]
         if kh == 0:
-            return pltpu.make_async_copy(s, e, tin.at[i, a])
-        return put(s, e, st.at[0, a], tin.at[i, a], (d, mp_of(hh)))
-
-    def up_w(i, a, cs):
-        s, e = WB[a].at[i, :, :, span(cs, rows)], WB[a].at[i, :, :, span(d, rows)]
-        return put(s, e, sw.at[1, a], wout.at[i, a], (base + cs, m))
-
-    def up_t(i, a, cs):
-        s, e = XB[a].at[i, :, span(cs, tok)], XB[a].at[i, :, span(slot, tok)]
-        return put(s, e, st.at[1, a], tin.at[i, a], (base + cs, m))
-
-    def relay_in(i, a, kh):
-        s = WB[a].at[i, (h + kh) % 4, :, span(base // nc, nc * rows)]
-        return put(s, s, sr.at[0, a], wrel.at[i, a], (other + core, m))
-
-    def relay_out(i, a):
-        s = WB[a].at[i, :, :, span(far // nc, nc * rows)]
-        return put(s, s, sr.at[1, a], wrel.at[i, a], (other + core, m))
+            return pltpu.make_async_copy(s, e, tin.at[i])
+        return put(s, e, st.at[a], tin.at[i], (d, mp_of(hh)))
+
+    def up_w(i, cs):
+        s, e = wb.at[i, :, :, span(cs, rows)], wb.at[i, :, :, span(d, rows)]
+        return put(s, e, sr.at[0], wout.at[i], (base + cs, m))
+
+    def up_t(i, cs):
+        s, e = xc.at[i, :, :, span(cs, tok)], xc.at[i, :, :, span(slot, tok)]
+        return put(s, e, sr.at[1], tin.at[i], (base + cs, m))
+
+    def relay_in(i, kh):
+        s = wb.at[i, (h + kh) % 4, :, span(base // nc, nc * rows)]
+        return put(s, s, sr.at[0], wrel.at[i], (other + core, m))
+
+    def relay_out(i):
+        s = wb.at[i, :, :, span(far // nc, nc * rows)]
+        return put(s, s, sr.at[1], wrel.at[i], (other + core, m))
 
     def tokens_out(i, k, more=0):
         u = (us + k) % n_o
@@ -275,19 +274,22 @@
             return pltpu.make_async_copy(s, e, done.at[0])
         return put(s, e, si.at[more], done.at[0], (first + u // 4, mp_of(u % 4)))
 
-    def partial(i, a, kh, near):
+    def sums(i, kh, near):
+        return gin.at[2 * i + near if i < ng - 1 else 2 * i + 4 * near + kh]
+
+    def partial(i, kh, near):
         hh, theirs = (h + kh) % 4, other // nc if near else 3 - far // nc
-        s = G[a].at[i, hh, :, span(theirs, nc * rows)]
-        return put(s, GI[a].at[i, hh, near], sg.at[a], gin.at[i, a, kh, near], (other + core, m))
-
-    def grads_out(i, a, kh, near, k):
+        s = g.at[i, hh, :, span(theirs, nc * rows)]
+        return put(s, gi.at[i, near, hh], sg, sums(i, kh, near), (other + core, m))
+
+    def grads_out(i, kh, near, k):
         hh, cs = (h + kh) % 4, (core + k) % nc
-        s, e = GI[a].at[i, hh, near, :, span(cs, rows)], GO[a].at[me * ng + i]
+        s, e = gi.at[i, near, hh, :, span(cs, rows)], go.at[me * ng + i]
         if near and kh == 0 and k == 0:
-            return pltpu.make_async_copy(s, e, done.at[1 + a])
-        return put(s, e, sf.at[near, a], done.at[1 + a], ((base if near else far) + cs, mp_of(hh)))
-
-    parts = [(a, kh, near) for near in (0, 1) for kh in (1, 2, 3, 0) for a in (0, 1)]
+            return pltpu.make_async_copy(s, e, done.at[1])
+        return put(s, e, sf.at[near], done.at[1], ((base if near else far) + cs, mp_of(hh)))
+
+    lasts = (1, 2, 3, 0)
 
     def both(f, *at):
         return [f(at[0], a, *at[1:]) for a in (0, 1)]
@@ -297,13 +299,17 @@
             copy.start()
 
     def combine(i):
-        for a, kh, near in parts:
-            hh = (h + kh) % 4
-            arrived(GI[a].at[i, hh, near], gin.at[i, a, kh, near])
-            ours = base // nc if near else far // nc
-            mine = G[a][i, hh, :, span(ours, nc * rows)].astype(jnp.float32)
-            GI[a][i, hh, near] = (mine + GI[a][i, hh, near].astype(jnp.float32)).astype(jnp.bfloat16)
-            begin([grads_out(i, a, kh, near, k) for k in range(nc)])
+        for near in (0, 1):
+            if i < ng - 1:
+                arrived(gi.at[i, near], sums(i, 0, near))
+            for kh in lasts:
+                hh = (h + kh) % 4
+                if i == ng - 1:
+                    arrived(gi.at[i, near, hh], sums(i, kh, near))
+                ours = base // nc if near else far // nc
+                mine = g[i, hh, :, span(ours, nc * rows)].astype(jnp.float32)
+                gi[i, near, hh] = (mine + gi[i, near, hh].astype(jnp.float32)).astype(jnp.bfloat16)
+                begin([grads_out(i, kh, near, k) for k in range(nc)])
 
     @pl.when(inner)
     def _():
@@ -318,23 +324,25 @@
             sweep(1, n_s, lambda k: begin(both(own_t, i, k)))
             begin(both(own_t, i, 0))
         for i in range(ng):
+            rest = span(base // nc, nc * rows)
+            if i:
+                arrived(wb.at[i, :, :, rest], win.at[3 + i])
             for kh in range(4):
-                for a in (0, 1):
-                    hh = (h + kh) % 4
-                    arrived(WB[a].at[i, hh, :, span(base // nc, nc * rows)], win.at[i, a, hh])
-                    if kh:
-                        relay_in(i, a, kh).start()
-        for i in range(ng):
-            for a in (0, 1):
-                arrived(WB[a].at[i, :, :, span(far // nc, nc * rows)], wout.at[i, a])
-                relay_out(i, a).start()
+                if i == 0:
+                    arrived(wb.at[i, (h + kh) % 4, :, rest], win.at[(h + kh) % 4])
+                if kh:
+                    relay_in(i, kh).start()
+        for i in range(ng):
+            arrived(wb.at[i, :, :, span(far // nc, nc * rows)], wout.at[i])
+            relay_out(i).start()
         arrived(order, ordered)
         for i in range(ng):
-            for a in (0, 1):
-                arrived(WB[a].at[i, :, :, span(1 - side, 2 * nc * rows)], wrel.at[i, a])
-                arrived(XB[a].at[i], tin.at[i, a])
-            factors(scale, order, xb.at[i], cb.at[i], w1b.at[i], w2b.at[i], ig.at[i], gf.at[i], gs.at[i], w1p, w2p, act, pre)
-            begin([partial(i, *at) for at in parts])
+            arrived(wb.at[i, :, :, span(1 - side, 2 * nc * rows)], wrel.at[i])
+            arrived(xc.at[i], tin.at[i])
+            w1b, w2b = wb.at[i, :, pl.ds(0, 2)], wb.at[i, :, pl.ds(2, 2)]
+            gf, gs = g.at[i, :, pl.ds(0, 2)], g.at[i, :, pl.ds(2, 2)]
+            factors(scale, order, xc.at[i, 0], xc.at[i, 1], w1b, w2b, ig.at[i], gf, gs, w1p, w2p, act, pre)
+            begin([partial(i, kh, near) for near in (0, 1) for kh in lasts])
             sweep(1, n_s, lambda k: tokens_out(i, k).start())
             sweep(n_s, n_o, lambda k: tokens_out(i, k, 1).start())
             tokens_out(i, 0).start()
@@ -345,14 +353,14 @@
         arrived(igo.at[:, pl.ds(0, some * B)], si.at[0])
         arrived(igo, si.at[1])
         for a in (0, 1):
-            arrived(X[a].at[:, pl.ds(0, some * B)], st.at[0, a])
+            arrived(X[a].at[:, pl.ds(0, some * B)], st.at[a])
             arrived(W[a].at[pl.ds(0, some)], sw.at[0, a])
             arrived(W[a].at[pl.ds(0, ng * nc)], sw.at[1, a])
-            arrived(WB[a].at[:, pl.ds(0, 3), :, pl.ds(0, nc * rows)], sr.at[0, a])
-            arrived(WB[a].at[:, :, :, pl.ds(0, nc * rows)], sr.at[1, a])
-            arrived(GI[a], sg.at[a])
-            arrived(GO[a], sf.at[0, a])
-            arrived(GO[a].at[pl.ds(0, some)], sf.at[1, a])
+        arrived(wb.at[:, pl.ds(0, 3), :, pl.ds(0, nc * rows)], sr.at[0])
+        arrived(wb.at[:, :, :, pl.ds(0, nc * rows)], sr.at[1])
+        arrived(gi, sg)
+        arrived(go, sf.at[0])
+        arrived(go.at[pl.ds(0, some)], sf.at[1])
 
     @pl.when(outer)
     def _():
@@ -365,22 +373,19 @@
                 for cs in range(nc):
                     begin(both(plane_t, i, cs, kh))
         for i in range(ng):
-            for a in (0, 1):
-                arrived(WB[a].at[i, :, :, span(0, nc * rows)], wout.at[i, a])
-                begin([up_w(i, a, cs) for cs in range(nc)])
-        for i in range(ng):
-            for a in (0, 1):
-                arrived(XB[a].at[i, :, span(0, nc * tok)], tin.at[i, a])
-                begin([up_t(i, a, cs) for cs in range(nc)])
+            arrived(wb.at[i, :, :, span(0, nc * rows)], wout.at[i])
+            begin([up_w(i, cs) for cs in range(nc)])
+        for i in range(ng):
+            arrived(xc.at[i, :, :, span(0, nc * tok)], tin.at[i])
+            begin([up_t(i, cs) for cs in range(nc)])
         for a in (0, 1):
             arrived(W[a].at[pl.ds(0, 3 * ng * nc)], sw.at[0, a])
-            arrived(X[a].at[:, pl.ds(0, 3 * ng * nc * B)], st.at[0, a])
-            arrived(W[a], sw.at[1, a])
-            arrived(X[a], st.at[1, a])
+            arrived(X[a].at[:, pl.ds(0, 3 * ng * nc * B)], st.at[a])
+        arrived(go, sr.at[0])
+        arrived(xc.at[:, :, :, pl.ds(0, nc * tok)], sr.at[1])
 
     arrived(igo, done.at[0])
-    arrived(gfo, done.at[1])
-    arrived(gso, done.at[2])
+    arrived(go, done.at[1])
 
 
 def by_lanes(plan, inputs, cotangent, first_weight, second_weight, orders):
@@ -389,54 +394,55 @@
     nc, ng, bf = plan.nc, plan.ng, jnp.bfloat16
     scale = 1.0 / math.sqrt(tok * 4 * nc)
     dma = pltpu.SemaphoreType.DMA
-    toks = pltpu.VMEM((ng, 4, 2 * nc * tok, B), bf)
-    mats = pltpu.VMEM((ng, 4, 2, B, B), bf)
-    half = pltpu.VMEM((ng, 4, 2, 2, nc * rows, B), bf)
-    part = pltpu.VMEM(first_weight.shape, bf)
-    input_grad, first, second = pl.pallas_call(
+    all_tok = 2 * nc * tok
+    mats = pltpu.VMEM((ng, 4, 4, B, B), bf)
+    input_grad, sums = pl.pallas_call(
         functools.partial(lanes, plan, scale),
-        out_shape=(pltpu.VMEM((tok, width), bf), part, part),
+        out_shape=(pltpu.VMEM((tok, width), bf), pltpu.VMEM((4 * nc * ng, 4, rows, B), bf)),
         in_specs=[ANY] * 5,
-        out_specs=(ANY,) * 3,
+        out_specs=(ANY,) * 2,
         scratch_shapes=[pltpu.VMEM(orders.shape, orders.dtype), dma]
-        + [toks, toks, mats, mats, toks, mats, mats, half, half]
+        + [pltpu.VMEM((ng, 2, 4, all_tok, B), bf), mats]
+        + [pltpu.VMEM((ng, 4, all_tok, B), bf), mats, pltpu.VMEM((ng, 2, 4, 4, nc * rows, B), bf)]
         + [pltpu.VMEM((4, B, B), bf)] * 2
-        + [pltpu.VMEM((4, 2 * nc * tok, B), bf)] * 2
-        + [dma((ng, 2)), dma((ng, 2, 4)), dma((ng, 2)), dma((ng, 2)), dma((ng, 2, 4, 2)), dma((3,))]
-        + [dma((2, 2))] * 3 + [dma((2,))] * 2 + [dma((2, 2))],
+        + [pltpu.VMEM((4, all_tok, B), bf)] * 2
+        + [dma((ng,)), dma((ng + 3,)), dma((ng,)), dma((ng,)), dma((2 * ng + 6,)), dma((2,))]
+        + [dma((2,)), dma((2, 2)), dma((2,)), dma((2,)), dma, dma((2,))],
         compiler_params=pltpu.CompilerParams(
             collective_id=0, has_side_effects=True, vmem_limit_bytes=58 * 2**20
         ),
         name="lanes",
     )(orders, inputs, cotangent, first_weight, second_weight)
-    return finish(input_grad, first, second)
-
-
-def store(ig, first, second, igo, fo, so, fw, sw, sems):
+    return finish(input_grad, sums)
+
+
+def store(ig, sums, igo, fo, so, fw, sw, sems):
     copies = [pltpu.make_async_copy(ig, igo, sems.at[0, 0])]
     copies[0].start()
-    size = max(1, first.shape[0] // CHUNKS)
-    for n, at in enumerate(range(0, first.shape[0], size)):
-        for a, (src, wide, dst) in enumerate(((first, fw, fo), (second, sw, so))):
+    size = max(1, sums.shape[0] // CHUNKS)
+    for n, at in enumerate(range(0, sums.shape[0], size)):
+        for a, (wide, dst) in enumerate(((fw, fo), (sw, so))):
             rows = pl.ds(at, size)
-            wide[rows] = src[rows].astype(jnp.float32)
+            wide[rows] = sums[rows, pl.ds(2 * a, 2)].astype(jnp.float32)
             copies.append(pltpu.make_async_copy(wide.at[rows], dst.at[rows], sems.at[1 + a, n]))
             copies[-1].start()
     for copy in copies:
         copy.wait()
 
 
-def finish(input_grad, first, second):
-    wide = jax.ShapeDtypeStruct(first.shape, jnp.float32)
+def finish(input_grad, sums):
+    nb, _, rows, width = sums.shape
+    wide = (nb, 2, rows, width)
+    out = jax.ShapeDtypeStruct(wide, jnp.float32)
     return pl.pallas_call(
         store,
-        out_shape=(jax.ShapeDtypeStruct(input_grad.shape, input_grad.dtype), wide, wide),
-        in_specs=[pl.BlockSpec(memory_space=pltpu.VMEM)] * 3,
+        out_shape=(jax.ShapeDtypeStruct(input_grad.shape, input_grad.dtype), out, out),
+        in_specs=[pl.BlockSpec(memory_space=pltpu.VMEM)] * 2,
         out_specs=(ANY,) * 3,
-        scratch_shapes=[pltpu.VMEM(first.shape, jnp.float32)] * 2 + [pltpu.SemaphoreType.DMA((3, CHUNKS))],
+        scratch_shapes=[pltpu.VMEM(wide, jnp.float32)] * 2 + [pltpu.SemaphoreType.DMA((3, CHUNKS))],
         compiler_params=pltpu.CompilerParams(vmem_limit_bytes=48 * 2**20),
         name="store",
-    )(input_grad, first, second)
+    )(input_grad, sums)
 
 
 def dot(left, right, dims=(((1,), (0,)), ((), ()))):

time: 191 us -> 191 us (level)
  no operation moved by 1% of the time
where the time goes in v6:
time: 191 us
  Pallas kernels  190 us (99%)
    pallas_call x1, Pallas kernels, by_lanes(): pl.pallas_call(functools.partial(lanes, plan, scale), out_shape=(pltpu.VM...  187 us

profile of v6, /device:TPU:9, one launch (start us, length us, event | category | flops | bytes accessed | tf_op | source)
XLA Modules:
  0.0 190.5 jit_solution(5946912103475317863)
XLA Ops:
  0.6 187.0 %lanes.1 = (bf16[128,8192]{1,0:T(8,128)(2,1)S(1)}, bf16[32,4,32,256]{3,2,1,0:T(8,128)(2,1)S(1)}) custom-call(s32[2,256]{1,0:T(2,128)} %orders.1, bf16[128,8192]{1,0:T(8,128)(2,1)} %x.1, bf16[128,8192]{1,0:T(8,128)(2,1)} %c.1, bf16[32,2,32,256]{3,2,1,0:T(8,128)(2,1)} %w1.1, bf16[32,2,32,256]{3,2,1,0:T(8,128)(2,1)} %w2.1), custom_call_target="tpu_custom_call" | custom-call | tf_op jit(solution)/shard_map/lanes/pallas_call | solution.py:399
  187.6 2.8 %store.1 = (bf16[128,8192]{1,0:T(8,128)(2,1)}, f32[32,2,32,256]{3,2,1,0:T(8,128)}, f32[32,2,32,256]{3,2,1,0:T(8,128)}) custom-call(bf16[128,8192]{1,0:T(8,128)(2,1)S(1)} %get-tuple-element.5.ig, bf16[32,4,32,256]{3,2,1,0:T(8,128)(2,1)S(1)} %get-tuple-element.6.sums), custom_call_target="tpu_custom_call" | custom-call | tf_op jit(solution)/shard_map/store/pallas_call | solution.py:437

commit v7 on v6

--- a/solution.py
+++ b/solution.py
@@ -179,6 +179,9 @@
     n_s, n_o = 4 * nc, 8 * nc
     X, W = (x, c), (w1, w2)
 
+    def column(kh):
+        return (h, h + 1 - 2 * (h % 2), (h + 2) % 4, 3 - h)[kh]
+
     def mp_of(hh):
         return hh * low + lo
 
@@ -210,7 +213,7 @@
     @pl.when(outer)
     def _():
         for kh in range(1, 4):
-            hello((d, mp_of((h + kh) % 4)))
+            hello((d, mp_of(column(kh))))
         pl.semaphore_wait(barrier, nc + 3)
 
     def block_of(a, t, i):
@@ -238,21 +241,24 @@
         return put(columns_of(a, t, i), e, st.at[a], tin.at[i], (base + t // 4, mp_of(t % 4)))
 
     def plane_w(i, a, cs, kh):
-        hh = (h + kh) % 4
+        hh = column(kh)
         s, e = block_of(a, cs * 4 + hh, i), wb.at[i, h, pl.ds(2 * a, 2), span(cs, rows)]
-        if kh == 0:
-            return pltpu.make_async_copy(s, e, wout.at[i])
         return put(s, e, sw.at[0, a], wout.at[i], (d, mp_of(hh)))
 
+    def straight_w(i, a, cs):
+        e = wb.at[i, h, pl.ds(2 * a, 2), span(d, rows)]
+        return put(block_of(a, cs * 4 + h, i), e, sw.at[1, a], wout.at[i], (base + cs, m))
+
     def plane_t(i, a, cs, kh):
-        hh = (h + kh) % 4
+        hh = column(kh)
         s, e = columns_of(a, cs * 4 + hh, i), xc.at[i, a, h, span(cs, tok)]
         if kh == 0:
             return pltpu.make_async_copy(s, e, tin.at[i])
         return put(s, e, st.at[a], tin.at[i], (d, mp_of(hh)))
 
-    def up_w(i, cs):
-        s, e = wb.at[i, :, :, span(cs, rows)], wb.at[i, :, :, span(d, rows)]
+    def up_w(i, cs, kh):
+        hh = column(kh)
+        s, e = wb.at[i, hh, :, span(cs, rows)], wb.at[i, hh, :, span(d, rows)]
         return put(s, e, sr.at[0], wout.at[i], (base + cs, m))
 
     def up_t(i, cs):
@@ -260,7 +266,7 @@
         return put(s, e, sr.at[1], tin.at[i], (base + cs, m))
 
     def relay_in(i, kh):
-        s = wb.at[i, (h + kh) % 4, :, span(base // nc, nc * rows)]
+        s = wb.at[i, column(kh), :, span(base // nc, nc * rows)]
         return put(s, s, sr.at[0], wrel.at[i], (other + core, m))
 
     def relay_out(i):
@@ -275,21 +281,33 @@
         return put(s, e, si.at[more], done.at[0], (first + u // 4, mp_of(u % 4)))
 
     def sums(i, kh, near):
-        return gin.at[2 * i + near if i < ng - 1 else 2 * i + 4 * near + kh]
+        return gin.at[2 * i + near]
 
     def partial(i, kh, near):
-        hh, theirs = (h + kh) % 4, other // nc if near else 3 - far // nc
+        hh, theirs = column(kh), other // nc if near else 3 - far // nc
         s = g.at[i, hh, :, span(theirs, nc * rows)]
         return put(s, gi.at[i, near, hh], sg, sums(i, kh, near), (other + core, m))
 
-    def grads_out(i, kh, near, k):
-        hh, cs = (h + kh) % 4, (core + k) % nc
-        s, e = gi.at[i, near, hh, :, span(cs, rows)], go.at[me * ng + i]
+    def partial_half(kh, near, half):
+        hh, theirs, two = column(kh), other // nc if near else 3 - far // nc, pl.ds(2 * half, 2)
+        s, e = g.at[ng - 1, hh, two, span(theirs, nc * rows)], gi.at[ng - 1, near, hh, two]
+        return put(s, e, sg, gin.at[2 * ng - 2 + 8 * near + 2 * kh + half], (other + core, m))
+
+    def own_rows(k):
+        cs = (core + 1 + k) % nc
+        s, e = g.at[ng - 1, h, :, span(other + cs, rows)], gi.at[ng - 1, 1, h, :, span(cs, rows)]
+        return put(s, e, sg, gin.at[2 * ng + 14 + k], (other + core, m))
+
+    def grads_out(i, kh, near, k, mats=slice(None)):
+        hh, cs = column(kh), (core + k) % nc
+        s, e = gi.at[i, near, hh, mats, span(cs, rows)], go.at[me * ng + i, mats]
         if near and kh == 0 and k == 0:
             return pltpu.make_async_copy(s, e, done.at[1])
         return put(s, e, sf.at[near], done.at[1], ((base if near else far) + cs, mp_of(hh)))
 
-    lasts = (1, 2, 3, 0)
+    lasts = (3, 1, 2, 0)
+    order_at_end = ((3, 0), (1, 0), (2, 0), (3, 1), (1, 1), (0, 0), (2, 1))
+    farthest_first = [(kh, near, half) for kh, near in order_at_end for half in (0, 1)]
 
     def both(f, *at):
         return [f(at[0], a, *at[1:]) for a in (0, 1)]
@@ -298,18 +316,35 @@
         for copy in copies:
             copy.start()
 
+    def add(i, kh, near, mats=slice(None)):
+        hh = column(kh)
+        ours = base // nc if near else far // nc
+        mine = g[i, hh, mats, span(ours, nc * rows)].astype(jnp.float32)
+        gi[i, near, hh, mats] = (mine + gi[i, near, hh, mats].astype(jnp.float32)).astype(jnp.bfloat16)
+        begin([grads_out(i, kh, near, k, mats) for k in range(nc)])
+
     def combine(i):
         for near in (0, 1):
-            if i < ng - 1:
-                arrived(gi.at[i, near], sums(i, 0, near))
+            arrived(gi.at[i, near], sums(i, 0, near))
             for kh in lasts:
-                hh = (h + kh) % 4
-                if i == ng - 1:
-                    arrived(gi.at[i, near, hh], sums(i, kh, near))
-                ours = base // nc if near else far // nc
-                mine = g[i, hh, :, span(ours, nc * rows)].astype(jnp.float32)
-                gi[i, near, hh] = (mine + gi[i, near, hh].astype(jnp.float32)).astype(jnp.bfloat16)
-                begin([grads_out(i, kh, near, k) for k in range(nc)])
+                add(i, kh, near)
+
+    def combine_last():
+        i = ng - 1
+        for kh, near, half in farthest_first:
+            two = pl.ds(2 * half, 2)
+            arrived(gi.at[i, near, column(kh), two], gin.at[2 * ng - 2 + 8 * near + 2 * kh + half])
+            add(i, kh, near, two)
+        for k in range(nc):
+            cs = (core + 1 + k) % nc
+            arrived(gi.at[i, 1, h, :, span(cs, rows)], gin.at[2 * ng + 14 + k])
+            mine = g[i, h, :, span(base + cs, rows)].astype(jnp.float32)
+            total = (mine + gi[i, 1, h, :, span(cs, rows)].astype(jnp.float32)).astype(jnp.bfloat16)
+            if k < nc - 1:
+                gi[i, 1, h, :, span(cs, rows)] = total
+                grads_out(i, 0, 1, 1 + k).start()
+            else:
+                go[me * ng + i] = total
 
     @pl.when(inner)
     def _():
@@ -329,7 +364,7 @@
                 arrived(wb.at[i, :, :, rest], win.at[3 + i])
             for kh in range(4):
                 if i == 0:
-                    arrived(wb.at[i, (h + kh) % 4, :, rest], win.at[(h + kh) % 4])
+                    arrived(wb.at[i, column(kh), :, rest], win.at[column(kh)])
                 if kh:
                     relay_in(i, kh).start()
         for i in range(ng):
@@ -342,13 +377,16 @@
             w1b, w2b = wb.at[i, :, pl.ds(0, 2)], wb.at[i, :, pl.ds(2, 2)]
             gf, gs = g.at[i, :, pl.ds(0, 2)], g.at[i, :, pl.ds(2, 2)]
             factors(scale, order, xc.at[i, 0], xc.at[i, 1], w1b, w2b, ig.at[i], gf, gs, w1p, w2p, act, pre)
-            begin([partial(i, kh, near) for near in (0, 1) for kh in lasts])
+            if i < ng - 1:
+                begin([partial(i, kh, near) for near in (0, 1) for kh in lasts])
+            else:
+                begin([partial_half(*at) for at in farthest_first] + [own_rows(k) for k in range(nc)])
             sweep(1, n_s, lambda k: tokens_out(i, k).start())
             sweep(n_s, n_o, lambda k: tokens_out(i, k, 1).start())
             tokens_out(i, 0).start()
             if i >= 1:
                 combine(i - 1)
-        combine(ng - 1)
+        combine_last()
         some = ng * (n_s - 1)
         arrived(igo.at[:, pl.ds(0, some * B)], si.at[0])
         arrived(igo, si.at[1])
@@ -361,11 +399,15 @@
         arrived(gi, sg)
         arrived(go, sf.at[0])
         arrived(go.at[pl.ds(0, some)], sf.at[1])
+        arrived(go.at[pl.ds(0, 4 * nc * ng - 1)], done.at[1])
 
     @pl.when(outer)
     def _():
         for i in range(ng):
-            for kh in (1, 2, 3, 0):
+            for cs in range(nc):
+                begin(both(straight_w, i, cs))
+        for i in range(ng):
+            for kh in (1, 2, 3):
                 for cs in range(nc):
                     begin(both(plane_w, i, cs, kh))
         for i in range(ng):
@@ -373,19 +415,20 @@
                 for cs in range(nc):
                     begin(both(plane_t, i, cs, kh))
         for i in range(ng):
-            arrived(wb.at[i, :, :, span(0, nc * rows)], wout.at[i])
-            begin([up_w(i, cs) for cs in range(nc)])
+            arrived(wb.at[i, pl.ds(0, 3), :, span(0, nc * rows)], wout.at[i])
+            begin([up_w(i, cs, kh) for kh in (1, 2, 3) for cs in range(nc)])
         for i in range(ng):
             arrived(xc.at[i, :, :, span(0, nc * tok)], tin.at[i])
             begin([up_t(i, cs) for cs in range(nc)])
         for a in (0, 1):
             arrived(W[a].at[pl.ds(0, 3 * ng * nc)], sw.at[0, a])
+            arrived(W[a].at[pl.ds(0, ng * nc)], sw.at[1, a])
             arrived(X[a].at[:, pl.ds(0, 3 * ng * nc * B)], st.at[a])
-        arrived(go, sr.at[0])
+        arrived(go.at[pl.ds(0, 3 * ng * nc)], sr.at[0])
         arrived(xc.at[:, :, :, pl.ds(0, nc * tok)], sr.at[1])
+        arrived(go, done.at[1])
 
     arrived(igo, done.at[0])
-    arrived(go, done.at[1])
 
 
 def by_lanes(plan, inputs, cotangent, first_weight, second_weight, orders):
@@ -400,13 +443,13 @@
         functools.partial(lanes, plan, scale),
         out_shape=(pltpu.VMEM((tok, width), bf), pltpu.VMEM((4 * nc * ng, 4, rows, B), bf)),
         in_specs=[ANY] * 5,
-        out_specs=(ANY,) * 2,
+        out_specs=(pl.BlockSpec(memory_space=pltpu.VMEM),) * 2,
         scratch_shapes=[pltpu.VMEM(orders.shape, orders.dtype), dma]
         + [pltpu.VMEM((ng, 2, 4, all_tok, B), bf), mats]
         + [pltpu.VMEM((ng, 4, all_tok, B), bf), mats, pltpu.VMEM((ng, 2, 4, 4, nc * rows, B), bf)]
         + [pltpu.VMEM((4, B, B), bf)] * 2
         + [pltpu.VMEM((4, all_tok, B), bf)] * 2
-        + [dma((ng,)), dma((ng + 3,)), dma((ng,)), dma((ng,)), dma((2 * ng + 6,)), dma((2,))]
+        + [dma((ng,)), dma((ng + 3,)), dma((ng,)), dma((ng,)), dma((2 * ng + 14 + nc,)), dma((2,))]
         + [dma((2,)), dma((2, 2)), dma((2,)), dma((2,)), dma, dma((2,))],
         compiler_params=pltpu.CompilerParams(
             collective_id=0, has_side_effects=True, vmem_limit_bytes=58 * 2**20

time: 191 us -> 190 us (level)
  no operation moved by 1% of the time
where the time goes in v7:
time: 190 us
  Pallas kernels  189 us (99%)
    pallas_call x1, Pallas kernels, by_lanes(): pl.pallas_call(functools.partial(lanes, plan, scale), out_shape=(pltpu.VM...  186 us

profile of v7, /device:TPU:9, one launch (start us, length us, event | category | flops | bytes accessed | tf_op | source)
XLA Modules:
  0.0 189.8 jit_solution(2117819182620949732)
XLA Ops:
  0.6 186.2 %lanes.1 = (bf16[128,8192]{1,0:T(8,128)(2,1)S(1)}, bf16[32,4,32,256]{3,2,1,0:T(8,128)(2,1)S(1)}) custom-call(s32[2,256]{1,0:T(2,128)} %orders.1, bf16[128,8192]{1,0:T(8,128)(2,1)} %x.1, bf16[128,8192]{1,0:T(8,128)(2,1)} %c.1, bf16[32,2,32,256]{3,2,1,0:T(8,128)(2,1)} %w1.1, bf16[32,2,32,256]{3,2,1,0:T(8,128)(2,1)} %w2.1), custom_call_target="tpu_custom_call" | custom-call | tf_op jit(solution)/shard_map/lanes/pallas_call | solution.py:442
  186.9 2.8 %store.1 = (bf16[128,8192]{1,0:T(8,128)(2,1)}, f32[32,2,32,256]{3,2,1,0:T(8,128)}, f32[32,2,32,256]{3,2,1,0:T(8,128)}) custom-call(bf16[128,8192]{1,0:T(8,128)(2,1)S(1)} %get-tuple-element.5.ig, bf16[32,4,32,256]{3,2,1,0:T(8,128)(2,1)S(1)} %get-tuple-element.6.sums), custom_call_target="tpu_custom_call" | custom-call | tf_op jit(solution)/shard_map/store/pallas_call | solution.py:480

commit v8 on v7

--- a/solution.py
+++ b/solution.py
@@ -203,12 +203,14 @@
     def _():
         for cs in range(nc):
             hello((other + cs, m))
-        for k in range(1, n_s):
-            t = (me + k) % n_s
-            hello((base + t // 4, mp_of(t % 4)))
+        for kh in (1, 2):
+            for cs in range(nc):
+                hello((base + cs, mp_of(column(kh))))
+        for k in range(1, nc):
+            hello((base + (core + k) % nc, m))
         for cs in range(nc):
             hello((far + cs, m))
-        pl.semaphore_wait(barrier, n_s - 1 + nc)
+        pl.semaphore_wait(barrier, 4 * nc - 1)
 
     @pl.when(outer)
     def _():
@@ -222,23 +224,23 @@
     def columns_of(a, t, i):
         return X[a].at[:, span(t * ng + i, B)]
 
-    def own_w(i, a, k):
-        t = (me + k) % n_s
-        e, arrival = wb.at[i, h, pl.ds(2 * a, 2), span(d, rows)], win.at[3 + i if i else h]
-        if isinstance(k, int) and k == 0:
-            return pltpu.make_async_copy(block_of(a, t, i), e, arrival)
-        return put(block_of(a, t, i), e, sw.at[0, a], arrival, (base + t // 4, mp_of(t % 4)))
+    def own_w(i, a, kh, k):
+        cs, hh = (core + k) % nc, column(kh)
+        s, e = block_of(a, cs * 4 + hh, i), wb.at[i, h, pl.ds(2 * a, 2), span(d, rows)]
+        if kh == 0 and k == 0:
+            return pltpu.make_async_copy(s, e, win.at[i, h])
+        return put(s, e, sw.at[0, a], win.at[i, h], (base + cs, mp_of(hh)))
 
     def cross_w(i, a, cs):
         e = wb.at[i, h, pl.ds(2 * a, 2), span(d, rows)]
         return put(block_of(a, cs * 4 + h, i), e, sw.at[1, a], wrel.at[i], (other + cs, m))
 
-    def own_t(i, a, k):
-        t = (me + k) % n_s
-        e = xc.at[i, a, h, span(slot, tok)]
-        if isinstance(k, int) and k == 0:
-            return pltpu.make_async_copy(columns_of(a, t, i), e, tin.at[i])
-        return put(columns_of(a, t, i), e, st.at[a], tin.at[i], (base + t // 4, mp_of(t % 4)))
+    def own_t(i, a, kh, k):
+        cs, hh = (core + k) % nc, column(kh)
+        s, e = columns_of(a, cs * 4 + hh, i), xc.at[i, a, h, span(slot, tok)]
+        if kh == 0 and k == 0:
+            return pltpu.make_async_copy(s, e, tin.at[i])
+        return put(s, e, st.at[a], tin.at[i], (base + cs, mp_of(hh)))
 
     def plane_w(i, a, cs, kh):
         hh = column(kh)
@@ -352,21 +354,26 @@
             for cs in range(nc):
                 begin(both(cross_w, i, cs))
         pltpu.make_async_copy(orders, order, ordered).start()
-        for i in range(ng):
-            sweep(1, n_s, lambda k: begin(both(own_w, i, k)))
-            begin(both(own_w, i, 0))
-        for i in range(ng):
-            sweep(1, n_s, lambda k: begin(both(own_t, i, k)))
-            begin(both(own_t, i, 0))
-        for i in range(ng):
-            rest = span(base // nc, nc * rows)
-            if i:
-                arrived(wb.at[i, :, :, rest], win.at[3 + i])
-            for kh in range(4):
-                if i == 0:
-                    arrived(wb.at[i, column(kh), :, rest], win.at[column(kh)])
-                if kh:
-                    relay_in(i, kh).start()
+        rest = span(base // nc, nc * rows)
+        for i in range(ng):
+            for kh in (1, 2, 0):
+                for k in range(nc):
+                    begin(both(own_w, i, kh, k))
+        arrived(wb.at[0, column(1), :, rest], win.at[0, column(1)])
+        relay_in(0, 1).start()
+        for i in range(ng):
+            for k in range(nc):
+                begin(both(own_w, i, 3, k))
+        for i in range(ng):
+            for kh in (3, 1, 2, 0):
+                for k in range(nc):
+                    begin(both(own_t, i, kh, k))
+        for kh in (1, 2, 3, 0):
+            for i in range(ng):
+                if i or kh != 1:
+                    arrived(wb.at[i, column(kh), :, rest], win.at[i, column(kh)])
+                    if kh:
+                        relay_in(i, kh).start()
         for i in range(ng):
             arrived(wb.at[i, :, :, span(far // nc, nc * rows)], wout.at[i])
             relay_out(i).start()
@@ -449,7 +456,7 @@
         + [pltpu.VMEM((ng, 4, all_tok, B), bf), mats, pltpu.VMEM((ng, 2, 4, 4, nc * rows, B), bf)]
         + [pltpu.VMEM((4, B, B), bf)] * 2
         + [pltpu.VMEM((4, all_tok, B), bf)] * 2
-        + [dma((ng,)), dma((ng + 3,)), dma((ng,)), dma((ng,)), dma((2 * ng + 14 + nc,)), dma((2,))]
+        + [dma((ng,)), dma((ng, 4)), dma((ng,)), dma((ng,)), dma((2 * ng + 14 + nc,)), dma((2,))]
         + [dma((2,)), dma((2, 2)), dma((2,)), dma((2,)), dma, dma((2,))],
         compiler_params=pltpu.CompilerParams(
             collective_id=0, has_side_effects=True, vmem_limit_bytes=58 * 2**20

time: 190 us -> 190 us (level)
  no operation moved by 1% of the time
where the time goes in v8:
time: 190 us
  Pallas kernels  189 us (99%)
    pallas_call x1, Pallas kernels, by_lanes(): pl.pallas_call(functools.partial(lanes, plan, scale), out_shape=(pltpu.VM...  186 us

profile of v8, /device:TPU:9, one launch (start us, length us, event | category | flops | bytes accessed | tf_op | source)
XLA Modules:
  0.0 189.8 jit_solution(16150021929307860748)
XLA Ops:
  0.6 186.2 %lanes.1 = (bf16[128,8192]{1,0:T(8,128)(2,1)S(1)}, bf16[32,4,32,256]{3,2,1,0:T(8,128)(2,1)S(1)}) custom-call(s32[2,256]{1,0:T(2,128)} %orders.1, bf16[128,8192]{1,0:T(8,128)(2,1)} %x.1, bf16[128,8192]{1,0:T(8,128)(2,1)} %c.1, bf16[32,2,32,256]{3,2,1,0:T(8,128)(2,1)} %w1.1, bf16[32,2,32,256]{3,2,1,0:T(8,128)(2,1)} %w2.1), custom_call_target="tpu_custom_call" | custom-call | tf_op jit(solution)/shard_map/lanes/pallas_call | solution.py:449
  186.8 2.8 %store.1 = (bf16[128,8192]{1,0:T(8,128)(2,1)}, f32[32,2,32,256]{3,2,1,0:T(8,128)}, f32[32,2,32,256]{3,2,1,0:T(8,128)}) custom-call(bf16[128,8192]{1,0:T(8,128)(2,1)S(1)} %get-tuple-element.5.ig, bf16[32,4,32,256]{3,2,1,0:T(8,128)(2,1)S(1)} %get-tuple-element.6.sums), custom_call_target="tpu_custom_call" | custom-call | tf_op jit(solution)/shard_map/store/pallas_call | solution.py:487
